TPU v7x, 128 devices: a whole 4x4x4 slice. The times are simulated.
128 devices in a mesh: rep: 16 (over z_hi, x, core), sp: 8 (over z_lo, y).
Axes of the slice: x: 4, y: 4, z: 4 (z_hi: 2, z_lo: 2; z = z_hi * 2 + z_lo), core: 2. Of those that a mesh axis runs over, the one named last changes fastest.
Arguments:
- positions: float32 [16, 3, 65536], P('rep', None, 'sp'), may hold values from -18 to 18
- velocities: float32 [16, 3, 65536], P('rep', None, 'sp'), may hold values from -6 to 6
- strength: float32 [16, 65536], P('rep', 'sp'), may hold values from 0.5 to 2
- inv_mass: float32 [16, 65536], P('rep', 'sp'), may hold values from 0.1 to 1
- tile_lists: int32 [16, 4, 512, 4], P('rep', None, 'sp'), may hold values from 0 to 127, as said below
- solute_index: int32 [16, 2048], P('rep', 'sp'), may hold values from 0 to 8191, as said below
- scatter_weight: float32 [16, 2048], P('rep', 'sp'), may hold values from 0.3 to 3
- intensity_exp: float32 [48], replicated, may hold values from 0.5 to 3
- precision: float32 [48], replicated, may hold values from 1 to 4
Outputs:
- positions_out: float32 [16, 3, 65536], P('rep', None, 'sp')
- velocities_out: float32 [16, 3, 65536], P('rep', None, 'sp')
Inputs may be any that keep to these rules, and one draw needn't show every extreme that they name: `tile_lists`: for each replica, step and local block b of a domain (numbered 0 to 63), the 4 entries are distinct extended block numbers from b to b + 64, among them b, b + 32 and b + 64. `solute_index`: within each replica and domain the 256 entries are distinct local atom numbers.
All inputs are finite; a program needn't handle non-finite values.
Results may differ from a plain program's by a relative error of at most 0.0001.
Values sent between devices are 32-bit elements; how exact they have to be, the bound alone decides.
No kernel may reach another device: no remote copies, remote signals or barrier semaphores. Data moves between devices by JAX's collectives and lax.ppermute only.
A program may use at most 128 MiB of HBM per device.

v0:
```python
import functools
import math

import jax
import jax.numpy as jnp
import numpy as np
from jax import lax
from jax.experimental import pallas as pl
from jax.experimental.pallas import tpu as pltpu
from jax.sharding import PartitionSpec as P

M = 784
NQ = 48
OUTER = 2
INNER = 2
TIME_STEP = 0.05
PAIR_STRENGTH = 0.2
HALF_INVERSE = 0.03125

BLOCK = 128
NB = 64
HB = 32
EXT = NB + 2 * HB
NEIGHBOURS = 4
ATOMS = NB * BLOCK
HALO = HB * BLOCK
SOL = 256
PARTS = 8
REPLICAS = 16
DIR_PART = M // PARTS
STEP_GROUPS = 7
STEPS = 2
GROUPS = STEPS * STEP_GROUPS
SIDE = 4
CENTERS = NQ // (2 * SIDE)
LANE_GROUPS = PARTS * SOL // 128
CHUNK = 4
FILL_UNROLL = 32
BLOCK_UNROLL = 16

ALPHA = math.sqrt(HALF_INVERSE * math.log2(math.e))
COUPLING = PAIR_STRENGTH / math.sqrt(NEIGHBOURS * BLOCK)
NORM = 1.0 / math.sqrt(PARTS * SOL)
TURN = 1.0 / (64.0 * math.pi)

F32 = jnp.float32
BF16 = jnp.bfloat16


def direction_table():
    order = np.arange(M)
    height = 1.0 - (2.0 * order + 1.0) / M
    radius = np.sqrt(1.0 - height * height)
    azimuth = (order * 610 % 987) * (2.0 * math.pi / 987.0)
    rows = np.stack([radius * np.cos(azimuth), radius * np.sin(azimuth), height], axis=-1) * TURN
    padded = np.zeros((PARTS, GROUPS * 8, 3), np.float32)
    padded[:, :DIR_PART] = rows.reshape(PARTS, DIR_PART, 3)
    table = np.zeros((PARTS, STEPS, 8, 128), np.float32)
    for c in range(3):
        part = padded[:, :, c].reshape(PARTS, STEPS, STEP_GROUPS, 8)
        table[:, :, :, 16 * c : 16 * c + STEP_GROUPS] = np.swapaxes(part, 2, 3)
    return table


def split3(value):
    high = value.astype(BF16).astype(F32)
    rest = value - high
    mid = rest.astype(BF16).astype(F32)
    return high, mid, rest - mid


def halves(value):
    high = value.astype(BF16)
    return high, (value - high.astype(F32)).astype(BF16)


def rows_of(shape):
    return lax.broadcasted_iota(jnp.int32, shape, 0)


def scaled_parts(cell, factor):
    row = rows_of((8, BLOCK))
    scaled = jnp.concatenate([cell, cell], axis=0) * ALPHA
    norm_row = (row & 3) == 3
    norm = -jnp.sum(jnp.where(row < 3, scaled * scaled, 0.0), axis=0, keepdims=True)
    return split3(jnp.where(norm_row, norm, scaled * factor))


def neighbour_features(cell):
    row = rows_of((8, BLOCK))
    both = jnp.concatenate([cell, cell], axis=0)
    charge = jnp.broadcast_to(cell[3:4], (8, BLOCK))
    moments = jnp.where((row & 3) == 3, charge, both * charge)
    th, tm, tl = split3(moments)
    weights = jnp.concatenate([jnp.where(row < 4, th, tm), jnp.where(row < 4, tl, 0.0)], axis=0)
    h, m, l = scaled_parts(cell, 1.0)
    near = [
        jnp.where((row & 3) == 3, 1.0, jnp.where(row < 4, h, m)),
        jnp.where(row < 3, l, jnp.where(row == 3, 1.0, h)),
        jnp.where(row < 4, m, jnp.where(row < 7, h, l)),
        jnp.zeros((8, BLOCK), F32),
    ]
    return jnp.concatenate(near, axis=0).astype(BF16), weights.astype(BF16)


def own_features(cell):
    row = rows_of((8, BLOCK))
    h, m, l = scaled_parts(cell, 2.0)
    own = [
        jnp.where(row == 7, m, h),
        jnp.where(row < 3, h, jnp.where(row == 3, l, jnp.where(row < 7, m, 1.0))),
        jnp.where((row & 3) == 3, 1.0, jnp.where(row < 4, m, l)),
        jnp.zeros((8, BLOCK), F32),
    ]
    return jnp.concatenate(own, axis=0).astype(BF16)


def selectors(index):
    block = lax.shift_right_logical(index, 7)
    lane = index & 127
    by_block = rows_of((NB, SOL)) == block
    by_lane = rows_of((BLOCK, SOL)) == lane
    return by_block, by_lane


def scatter_kicks(index_ref, weight_ref, kick_ref, push_ref):
    by_block, by_lane = selectors(index_ref[...])
    total = kick_ref[0]
    for part in range(1, PARTS):
        total = total + kick_ref[part]
    total = total * (weight_ref[...] * (-INNER * TIME_STEP))
    lanes = jnp.where(by_lane, 1.0, 0.0).astype(BF16)
    lanes = jnp.concatenate([lanes, lanes, lanes], axis=1)
    for c in range(3):
        parts = split3(total[c : c + 1])
        rows = jnp.concatenate([jnp.where(by_block, p, 0.0).astype(BF16) for p in parts], axis=1)
        push_ref[c] = lax.dot_general(rows, lanes, (((1,), (1,)), ((), ())), preferred_element_type=F32)


def gather_points(index_ref, weight_ref, place_ref, point_ref):
    by_block, by_lane = selectors(index_ref[...])
    lanes = jnp.where(by_lane, 1.0, 0.0).astype(BF16)
    found = []
    for c in range(3):
        total = None
        for p in split3(place_ref[c]):
            part = jnp.dot(p.astype(BF16), lanes, preferred_element_type=F32)
            total = part if total is None else total + part
        found.append(jnp.sum(jnp.where(by_block, total, 0.0), axis=0, keepdims=True))
    found.append(weight_ref[...])
    points = jnp.concatenate(found, axis=0)
    for part in range(PARTS):
        point_ref[part] = points


def block_at(b):
    return pl.ds(pl.multiple_of(b * BLOCK, BLOCK), BLOCK)


def pushed(push_ref, b):
    return jnp.concatenate([push_ref[c, pl.ds(b, 1), :] for c in range(3)], axis=0)


def pack_kernel(pos_ref, charge_ref, vel_ref, inverse_ref, index_ref, weight_ref, *refs):
    out_ref, head_ref, tail_ref, point_ref, place_ref = refs

    def one_block(b, carry):
        at = block_at(b)
        place = pos_ref[:, at]
        out_ref[:, at] = jnp.concatenate([place, charge_ref[:, at], vel_ref[:, at], inverse_ref[:, at]], axis=0)
        for c in range(3):
            place_ref[c, pl.ds(b, 1), :] = place[c : c + 1]
        return carry

    lax.fori_loop(0, NB, one_block, 0, unroll=FILL_UNROLL)
    head_ref[...] = out_ref[0:4, 0:HALO]
    tail_ref[...] = out_ref[0:4, HALO:ATOMS]
    gather_points(index_ref, weight_ref, place_ref, point_ref)


def finish_kernel(vel_ref, inverse_ref, index_ref, weight_ref, kick_ref, out_ref, push_ref):
    scatter_kicks(index_ref, weight_ref, kick_ref, push_ref)

    def one_block(b, carry):
        at = block_at(b)
        out_ref[:, at] = vel_ref[:, at] + inverse_ref[:, at] * pushed(push_ref, b)
        return carry

    lax.fori_loop(0, NB, one_block, 0, unroll=FILL_UNROLL)


def pair_kernel(step, kicked, gathers, last, *refs):
    refs = list(refs)
    fourth_ref, position_ref, state_ref, left_ref, right_ref = refs[:5]
    refs = refs[5:]
    if kicked or gathers:
        index_ref, weight_ref = refs[:2]
        refs = refs[2:]
    if kicked:
        kick_ref = refs.pop(0)
    if last:
        pos_ref, vel_ref = refs[:2]
        refs = refs[2:]
    else:
        out_ref, head_ref, tail_ref = refs[:3]
        refs = refs[3:]
    if gathers:
        point_ref = refs.pop(0)
    near_ref, moment_ref = refs[:2]
    refs = refs[2:]
    if gathers:
        place_ref = refs.pop(0)
    if kicked:
        push_ref = refs.pop(0)

    left_ok = jnp.where(position_ref[0] > 0, 1.0, 0.0)
    right_ok = jnp.where(position_ref[0] < PARTS - 1, 1.0, 0.0)
    row4 = rows_of((4, BLOCK))

    def fill(slot, cell):
        near, moments = neighbour_features(cell)
        near_ref[slot] = near.T
        moment_ref[slot] = moments

    def fill_halo(b, carry):
        at = block_at(b)
        fill(b, left_ref[:, at] * jnp.where(row4 == 3, left_ok, 1.0))
        fill(b + HB + NB, right_ref[:, at] * jnp.where(row4 == 3, right_ok, 1.0))
        return carry

    lax.fori_loop(0, HB, fill_halo, 0, unroll=FILL_UNROLL)

    def fill_own(b, carry):
        cell = state_ref[0:4, block_at(b)]
        fill(b + HB, cell)
        return carry

    lax.fori_loop(0, NB, fill_own, 0, unroll=FILL_UNROLL)

    if kicked:
        scatter_kicks(index_ref, weight_ref, kick_ref, push_ref)

    def update(b, cell, sums):
        sums = sums[0:4] + sums[4:8] + sums[8:12]
        at = block_at(b)
        place, charge, speed, inverse = cell[0:3], cell[3:4], cell[4:7], cell[7:8]
        force = (COUPLING * charge) * (place * sums[3:4] - sums[0:3])
        if kicked:
            speed = speed + inverse * pushed(push_ref, b)
        speed = speed + (TIME_STEP * inverse) * force
        place = place + TIME_STEP * speed
        if gathers:
            for c in range(3):
                place_ref[c, pl.ds(b, 1), :] = place[c : c + 1]
        if last:
            pos_ref[:, at] = place
            vel_ref[:, at] = speed
        else:
            out_ref[:, at] = jnp.concatenate([place, charge, speed, inverse], axis=0)

    def weighted(first, second, own):
        near = jnp.concatenate([near_ref[first], near_ref[second]], axis=0)
        moments = jnp.concatenate([moment_ref[first], moment_ref[second]], axis=1)
        high, low = halves(jnp.exp2(jnp.dot(near, own, preferred_element_type=F32)))
        sums = jnp.dot(moments, high, preferred_element_type=F32)
        return sums + jnp.dot(moments, low, preferred_element_type=F32)

    def one_pair(b, carry):
        c = b + HB
        cells = [state_ref[:, block_at(b)], state_ref[:, block_at(c)]]
        own = [own_features(v[0:4]) for v in cells]
        shared = weighted(b + HB, b + 2 * HB, jnp.concatenate(own, axis=1))
        left = weighted(b, fourth_ref[step * NB + b], own[0])
        right = weighted(b + 3 * HB, fourth_ref[step * NB + c], own[1])
        update(b, cells[0], shared[:, 0:BLOCK] + left)
        update(c, cells[1], shared[:, BLOCK:] + right)
        return carry

    lax.fori_loop(0, HB, one_pair, 0, unroll=BLOCK_UNROLL)

    if not last:
        head_ref[...] = out_ref[0:4, 0:HALO]
        tail_ref[...] = out_ref[0:4, HALO:ATOMS]
    if gathers:
        gather_points(index_ref, weight_ref, place_ref, point_ref)


VMEM = pl.BlockSpec(memory_space=pltpu.VMEM)
SMEM = pl.BlockSpec(memory_space=pltpu.SMEM)
PARAMS = pltpu.CompilerParams(vmem_limit_bytes=32 << 20)


def pack(positions, strength, velocities, inv_mass, index, weights):
    return pl.pallas_call(
        pack_kernel,
        out_shape=[
            jax.ShapeDtypeStruct((8, ATOMS), F32),
            jax.ShapeDtypeStruct((4, HALO), F32),
            jax.ShapeDtypeStruct((4, HALO), F32),
            jax.ShapeDtypeStruct((PARTS, 4, SOL), F32),
        ],
        in_specs=[VMEM] * 6,
        out_specs=[VMEM] * 4,
        scratch_shapes=[pltpu.VMEM((3, NB, BLOCK), F32)],
        compiler_params=PARAMS,
        cost_estimate=pl.CostEstimate(flops=100_000_000, bytes_accessed=600_000, transcendentals=0),
        name="pack",
    )(positions, strength, velocities, inv_mass, index, weights)


def finish(velocities, inv_mass, index, weights, kick):
    return pl.pallas_call(
        finish_kernel,
        out_shape=jax.ShapeDtypeStruct((3, ATOMS), F32),
        in_specs=[VMEM] * 5,
        out_specs=VMEM,
        scratch_shapes=[pltpu.VMEM((3, NB, BLOCK), F32)],
        compiler_params=PARAMS,
        cost_estimate=pl.CostEstimate(flops=100_000_000, bytes_accessed=300_000, transcendentals=0),
        name="finish",
    )(velocities, inv_mass, index, weights, kick)


def pair_step(step, tiles, position, state, halo, index=None, weights=None, kick=None, gathers=False, last=False):
    kicked = kick is not None
    operands = [tiles, position, state, halo[0], halo[1]]
    specs = [SMEM, SMEM, VMEM, VMEM, VMEM]
    if kicked or gathers:
        operands += [index, weights]
        specs += [VMEM, VMEM]
    if kicked:
        operands.append(kick)
        specs.append(VMEM)
    scratch = [
        pltpu.VMEM((EXT, BLOCK, 32), BF16),
        pltpu.VMEM((EXT, 16, BLOCK), BF16),
    ]
    if last:
        shapes = [jax.ShapeDtypeStruct((3, ATOMS), F32)] * 2
    else:
        shapes = [jax.ShapeDtypeStruct((8, ATOMS), F32)] + [jax.ShapeDtypeStruct((4, HALO), F32)] * 2
    if gathers:
        shapes.append(jax.ShapeDtypeStruct((PARTS, 4, SOL), F32))
        scratch.append(pltpu.VMEM((3, NB, BLOCK), F32))
    if kicked:
        scratch.append(pltpu.VMEM((3, NB, BLOCK), F32))
    return pl.pallas_call(
        functools.partial(pair_kernel, step, kicked, gathers, last),
        out_shape=shapes,
        in_specs=specs,
        out_specs=[VMEM] * len(shapes),
        scratch_shapes=scratch,
        compiler_params=PARAMS,
        cost_estimate=pl.CostEstimate(flops=6_000_000_000, bytes_accessed=2_000_000, transcendentals=4_000_000),
        name="pair_step",
    )(*operands)


def double(cos, sin):
    twice = sin + sin
    return 1.0 - twice * sin, twice * cos


def product(a, b):
    return a[0] * b[0] - a[1] * b[1], a[1] * b[0] + a[0] * b[1]


def product_conj(a, b):
    return a[0] * b[0] + a[1] * b[1], a[1] * b[0] - a[0] * b[1]


def unit_powers(turns):
    y = (turns - jnp.round(turns)) * (0.5 * math.pi)
    z = y * y
    sin = ((-1.9515295891e-4 * z + 8.3321608736e-3) * z - 1.6666654611e-1) * (z * y) + y
    cos = ((2.443315711809948e-5 * z - 1.388731625493765e-3) * z + 4.166664568298827e-2) * (z * z) + (1.0 - 0.5 * z)
    one = double(*double(cos, sin))
    two = double(*one)
    three = product(two, one)
    five = product(three, two)
    seven = product(five, two)
    sixteen = double(*double(*double(*two)))
    return [one, three, five, seven], sixteen, product(double(*sixteen), seven)


def term_rows(powers):
    values = [p[0] for p in powers] + [p[1] for p in powers]
    parts = [halves(jnp.concatenate(values[i : i + 2], axis=0)) for i in range(0, 8, 2)]
    return [p[0] for p in parts], [p[1] for p in parts]


def group_directions(dir_ref, group):
    return [jnp.broadcast_to(dir_ref[0, 0, :, 16 * c + group : 16 * c + group + 1], (8, 128)) for c in range(3)]


def group_turns(u, point_ref, part, half):
    lanes = slice(half * 128, half * 128 + 128)

    def coordinate(c):
        return jnp.broadcast_to(point_ref[part, c : c + 1, lanes], (8, 128))

    return u[0] * coordinate(0) + u[1] * coordinate(1) + u[2] * coordinate(2), coordinate(3)


def shell_of(down, k, o):
    return 8 * k + 3 - o if down else 8 * k + 4 + o


def amplitude_kernel(position_ref, point_ref, dir_ref, amp_ref, inten_ref, total_ref):
    row = rows_of((8, 128))
    lane = lax.broadcasted_iota(jnp.int32, (8, 128), 1)

    turn = pl.program_id(0)
    for group in range(STEP_GROUPS):
        u = group_directions(dir_ref, group)
        total = None
        for at in range(LANE_GROUPS // CHUNK):
            left = []
            right = []
            for n in range(CHUNK):
                j = at * CHUNK + n
                turns, weight = group_turns(u, point_ref, j // 2, j % 2)
                powers, step, start = unit_powers(turns)
                high, low = term_rows(powers)
                right.append(jnp.concatenate(high + low, axis=0))
                c, s = weight * start[0], weight * start[1]
                cb, sb = product_conj((c, s), step)
                twice = step[0] + step[0]
                tops = []
                bottoms = []
                for k in range(CENTERS):
                    top, bottom = halves(jnp.concatenate([c, s], axis=0))
                    tops.append(top)
                    bottoms.append(bottom)
                    if k + 1 < CENTERS:
                        c, s, cb, sb = twice * c - cb, twice * s - sb, c, s
                left.append(jnp.concatenate(tops + bottoms, axis=0))
            part = lax.dot_general(
                jnp.concatenate(left, axis=1),
                jnp.concatenate(right, axis=1),
                (((1,), (1,)), ((), ())),
                preferred_element_type=F32,
            )
            total = part if total is None else total + part
        total_ref[turn * STEP_GROUPS + group] = total[0 : 16 * CENTERS] + total[16 * CENTERS :]

    @pl.when(turn == STEPS - 1)
    def _():
        own = (lane & 7) == row
        front = lane < 8 * SIDE
        squares = [jnp.zeros((8, 128), F32)] * 2
        for g in range(GROUPS):
            real = jnp.zeros((8, 128), F32)
            imag = real
            for k in range(CENTERS):
                c = jnp.sum(jnp.where(own, total_ref[g, 16 * k : 16 * k + 8], 0.0), axis=0, keepdims=True)
                s = jnp.sum(jnp.where(own, total_ref[g, 16 * k + 8 : 16 * k + 16], 0.0), axis=0, keepdims=True)
                real = jnp.where(row == k, c, real)
                imag = jnp.where(row == k, s, imag)
            real = (real + pltpu.roll(real, 64, axis=1)) * NORM
            imag = (imag + pltpu.roll(imag, 64, axis=1)) * NORM
            real_sin = pltpu.roll(real, 96, axis=1)
            imag_sin = pltpu.roll(imag, 96, axis=1)
            planes = [real - imag_sin, real + imag_sin, imag + real_sin, imag - real_sin]
            inside = front & ((lane & 7) + g * 8 < DIR_PART)
            planes = [jnp.where(inside, p, 0.0) for p in planes]
            for i in range(4):
                amp_ref[g, i] = planes[i]
            for i in range(2):
                squares[i] = squares[i] + planes[i] * planes[i] + planes[i + 2] * planes[i + 2]
        spread = jnp.zeros((1, 128), F32)
        for i in range(2):
            square = squares[i]
            for shift in (1, 2, 4):
                square = square + pltpu.roll(square, 128 - shift, axis=1)
            for k in range(CENTERS):
                for o in range(SIDE):
                    spread = jnp.where(lane[0:1] == shell_of(i, k, o), square[k : k + 1, 8 * o : 8 * o + 1], spread)
        inten_ref[...] = jnp.broadcast_to(spread, inten_ref.shape)


def point_spec():
    return pl.BlockSpec((PARTS, 4, SOL), lambda g, p: (0, 0, 0))


def direction_spec():
    return pl.BlockSpec((1, 1, 8, 128), lambda g, p: (p[0], g, 0, 0))


def amplitudes(position, points, directions):
    return pl.pallas_call(
        amplitude_kernel,
        grid_spec=pltpu.PrefetchScalarGridSpec(
            num_scalar_prefetch=1,
            grid=(STEPS,),
            in_specs=[point_spec(), direction_spec()],
            out_specs=[
                pl.BlockSpec((GROUPS, 4, 8, 128), lambda g, p: (0, 0, 0, 0)),
                pl.BlockSpec((PARTS * REPLICAS, 128), lambda g, p: (0, 0)),
            ],
            scratch_shapes=[pltpu.VMEM((GROUPS, 16 * CENTERS, 128), F32)],
        ),
        out_shape=[
            jax.ShapeDtypeStruct((GROUPS, 4, 8, 128), F32),
            jax.ShapeDtypeStruct((PARTS * REPLICAS, 128), F32),
        ],
        compiler_params=PARAMS,
        cost_estimate=pl.CostEstimate(flops=10_000_000_000, bytes_accessed=1_000_000, transcendentals=0),
        name="amplitudes",
    )(position, points, directions)


def kick_kernel(position_ref, point_ref, dir_ref, amp_ref, inten_ref, precision_ref, target_ref, out_ref, coef_ref, acc_ref):
    row = rows_of((8, 128))
    lane = lax.broadcasted_iota(jnp.int32, (8, 128), 1)

    @pl.when(pl.program_id(0) == 0)
    def _():
        intensity = jnp.sum(inten_ref[...], axis=0, keepdims=True) * (1.0 / (M * REPLICAS))
        q = 1.0 + lax.broadcasted_iota(jnp.int32, (1, NQ), 1).astype(F32) * (3.0 / NQ)
        factor = precision_ref[...] * (intensity[:, 0:NQ] - target_ref[...]) * (2.0 / M) * q
        scales = []
        for i in range(2):
            scale = jnp.zeros((8, 128), F32)
            for k in range(CENTERS):
                for o in range(SIDE):
                    source = shell_of(i, k, o)
                    here = (row == k) & (lax.shift_right_logical(lane, 3) == o)
                    scale = jnp.where(here, jnp.broadcast_to(factor[:, source : source + 1], (8, 128)), scale)
            scales.append(scale)
        front = lane < 8 * SIDE
        own = (lane & 7) == row
        for g in range(GROUPS):
            b_up = amp_ref[g, 0] * scales[0]
            b_down = amp_ref[g, 1] * scales[1]
            a_up = amp_ref[g, 2] * scales[0]
            a_down = amp_ref[g, 3] * scales[1]
            real = jnp.where(front, a_up + a_down, pltpu.roll(b_down - b_up, 32, axis=1))
            imag = jnp.where(front, b_up + b_down, pltpu.roll(a_up - a_down, 32, axis=1))
            tops = []
            bottoms = []
            for v in (real, imag):
                high = v.astype(BF16).astype(F32)
                tops.append(high + pltpu.roll(high, 64, axis=1))
                bottoms.append(v - high)
            for k in range(CENTERS):
                at = slice(16 * k, 16 * k + 16)
                first = jnp.concatenate([jnp.where(own, v[k : k + 1], 0.0) for v in tops], axis=0).astype(BF16)
                last = jnp.concatenate([jnp.where(own, v[k : k + 1], 0.0) for v in bottoms], axis=0).astype(BF16)
                coef_ref[g, at, 0:128] = first
                coef_ref[g, at, 128:256] = last

    kicked = [[None] * 3 for _ in range(LANE_GROUPS)]
    turn = pl.program_id(0)
    for group in range(STEP_GROUPS):
        u = group_directions(dir_ref, group)

        for at in range(LANE_GROUPS // CHUNK):
            state = []
            columns = []
            for n in range(CHUNK):
                j = at * CHUNK + n
                turns, _ = group_turns(u, point_ref, j // 2, j % 2)
                powers, step, start = unit_powers(turns)
                high, low = term_rows(powers)
                columns.append(jnp.concatenate(high + low + high, axis=0))
                state.append([step, start, step[0] + step[0]])
            terms = jnp.dot(coef_ref[turn * STEP_GROUPS + group, :, 0:192], jnp.concatenate(columns, axis=1), preferred_element_type=F32)
            for n in range(CHUNK):
                step, start, twice = state[n]
                lanes = slice(n * 128, n * 128 + 128)
                r1 = i1 = r2 = i2 = None
                for k in range(CENTERS - 1, -1, -1):
                    real = terms[16 * k : 16 * k + 8, lanes]
                    imag = terms[16 * k + 8 : 16 * k + 16, lanes]
                    if r1 is not None:
                        real = real + twice * r1
                        imag = imag + twice * i1
                    if r2 is not None:
                        real = real - r2
                        imag = imag - i2
                    r1, i1, r2, i2 = real, imag, r1, i1
                real = r1 - r2 * step[0] - i2 * step[1]
                imag = i1 - i2 * step[0] + r2 * step[1]
                slope = real * start[0] - imag * start[1]
                for c in range(3):
                    value = u[c] * slope
                    old = kicked[at * CHUNK + n][c]
                    kicked[at * CHUNK + n][c] = value if old is None else old + value

    @pl.when(turn == 0)
    def _():
        for j in range(LANE_GROUPS):
            for c in range(3):
                acc_ref[3 * j + c] = kicked[j][c]

    @pl.when(turn == STEPS - 1)
    def _():
        for j in range(LANE_GROUPS):
            lanes = slice(j % 2 * 128, j % 2 * 128 + 128)
            for c in range(3):
                total = acc_ref[3 * j + c] + kicked[j][c]
                out_ref[j // 2, c : c + 1, lanes] = jnp.sum(total, axis=0, keepdims=True) * (1.0 / TURN)


def kicks(position, points, directions, amplitude, intensity, shells):
    return pl.pallas_call(
        kick_kernel,
        grid_spec=pltpu.PrefetchScalarGridSpec(
            num_scalar_prefetch=1,
            grid=(STEPS,),
            in_specs=[
                point_spec(),
                direction_spec(),
                pl.BlockSpec((GROUPS, 4, 8, 128), lambda g, p: (0, 0, 0, 0)),
                pl.BlockSpec((PARTS * REPLICAS, 128), lambda g, p: (0, 0)),
                pl.BlockSpec((1, NQ), lambda g, p: (0, 0)),
                pl.BlockSpec((1, NQ), lambda g, p: (0, 0)),
            ],
            out_specs=pl.BlockSpec((PARTS, 3, SOL), lambda g, p: (0, 0, 0)),
            scratch_shapes=[
                pltpu.VMEM((GROUPS, 16 * CENTERS, 256), BF16),
                pltpu.VMEM((LANE_GROUPS * 3, 8, 128), F32),
            ],
        ),
        out_shape=jax.ShapeDtypeStruct((PARTS, 3, SOL), F32),
        compiler_params=PARAMS,
        cost_estimate=pl.CostEstimate(flops=10_000_000_000, bytes_accessed=1_000_000, transcendentals=0),
        name="kicks",
    )(position, points, directions, amplitude, intensity, *shells)


def exchange(head, tail):
    right = [(i, (i + 1) % PARTS) for i in range(PARTS)]
    left = [((i + 1) % PARTS, i) for i in range(PARTS)]
    return lax.ppermute(tail, "sp", right), lax.ppermute(head, "sp", left)


def to_all(value, axes):
    return lax.all_to_all(value, axes, 0, 0, tiled=True)


def shards(
    positions,
    velocities,
    strength,
    inv_mass,
    tile_lists,
    solute_index,
    scatter_weight,
    intensity_exp,
    precision,
):
    position = lax.axis_index("sp").astype(jnp.int32).reshape(1)
    directions = jnp.asarray(direction_table())
    usual = 3 * (jnp.arange(NB, dtype=jnp.int32) + HB)
    tiles = (jnp.sum(tile_lists[0], axis=-1) - usual).reshape(-1)
    shells = (precision.reshape(1, NQ), intensity_exp.reshape(1, NQ))
    state, head, tail, first = pack(
        positions[0], strength, velocities[0], inv_mass, solute_index, scatter_weight
    )
    halo = exchange(head, tail)
    first, halo = lax.optimization_barrier((first, halo))
    first = to_all(first, "sp")
    state, head, tail = pair_step(0, tiles, position, state, halo)
    halo = exchange(head, tail)
    amp, inten = amplitudes(position, first, directions)
    inten = to_all(inten, ("rep", "sp"))
    state, head, tail, second = pair_step(
        1, tiles, position, state, halo, solute_index, scatter_weight, gathers=True
    )
    halo = exchange(head, tail)
    second = to_all(second, "sp")
    kick = to_all(kicks(position, first, directions, amp, inten, shells), "sp")
    amp, inten = amplitudes(position, second, directions)
    inten = to_all(inten, ("rep", "sp"))
    state, head, tail = pair_step(2, tiles, position, state, halo, solute_index, scatter_weight, kick)
    halo = exchange(head, tail)
    kick = to_all(kicks(position, second, directions, amp, inten, shells), "sp")
    place, speed = pair_step(3, tiles, position, state, halo, last=True)
    speed = finish(speed, inv_mass, solute_index, scatter_weight, kick)
    return (place[None], speed[None])


def solution(mesh):
    in_specs = (
        P("rep", None, "sp"),
        P("rep", None, "sp"),
        P("rep", "sp"),
        P("rep", "sp"),
        P("rep", None, "sp", None),
        P("rep", "sp"),
        P("rep", "sp"),
        P(),
        P(),
    )
    out_specs = (P("rep", None, "sp"), P("rep", None, "sp"))
    return jax.shard_map(shards, mesh=mesh, in_specs=in_specs, out_specs=out_specs, check_vma=False)
```

profile of v0, /device:TPU:8, one launch (start us, length us, event | category | flops | bytes accessed | tf_op | source)
XLA Modules:
  0.0 119.1 jit_solution(16511702263540972376)
XLA Ops:
  0.6 0.0 copy-start.1
  0.6 0.0 copy-start
  0.7 0.0 copy-start.3
  0.7 1.1 copy_bitcast_fusion
  1.8 0.0 copy-start.2
  1.8 0.0 copy-done.1
  1.8 0.0 copy-done
  1.8 0.0 copy-done.3
  1.8 0.6 copy-done.2
  2.4 0.0 copy-start.7
  2.4 1.0 pack.1
  3.5 1.6 %collective-permute-start = (f32[4,4096]{1,0:T(4,128)S(1)}, f32[4,4096]{1,0:T(4,128)S(1)}, u32[]{:S(2)}, u32[]{:S(2)}) collective-permute-start(f32[4,4096]{1,0:T(4,128)S(1)} %get-tuple-element.27), channel_id=1, source_target_pairs={{0,1},{1,2},{2,3},{3,4},{4,5},{5,6},{6,7},{7,0},{8,9},{9,10},{10,1... | collective-permute-start | bytes 196616 | tf_op jit(solution)/shard_map/ppermute | solution.py:636
  5.0 0.4 collective-permute-start.1
  5.5 0.0 copy-done.7
  5.5 0.1 sub.14.refs_0_
  5.6 2.1 %collective-permute-done.refs_3_ = f32[4,4096]{1,0:T(4,128)S(1)} collective-permute-done((f32[4,4096]{1,0:T(4,128)S(1)}, f32[4,4096]{1,0:T(4,128)S(1)}, u32[]{:S(2)}, u32[]{:S(2)}) %collective-permute-start) | collective-permute-done | bytes 65568 | tf_op jit(solution)/shard_map/ppermute | solution.py:636
  7.7 1.6 %collective-permute-done.1.refs_4_ = f32[4,4096]{1,0:T(4,128)S(1)} collective-permute-done((f32[4,4096]{1,0:T(4,128)S(1)}, f32[4,4096]{1,0:T(4,128)S(1)}, u32[]{:S(2)}, u32[]{:S(2)}) %collective-permute-start.1) | collective-permute-done | bytes 65568 | tf_op jit(solution)/shard_map/ppermute | solution.py:636
  9.3 6.8 %all-to-all-start = ((f32[8,4,256]{2,1,0:T(4,128)}), f32[8,4,256]{2,1,0:T(4,128)S(1)}, u32[]{:S(2)}, u32[]{:S(2)}) async-start(f32[8,4,256]{2,1,0:T(4,128)} %get-tuple-element.37), calls=%async_computation | async-start | bytes 65536 | tf_op jit(solution)/shard_map/all_to_all | solution.py:640
  16.2 0.0 copy-start.6
  16.2 7.0 %pair_step.4 = (f32[8,8192]{1,0:T(8,128)S(1)}, f32[4,4096]{1,0:T(4,128)S(1)}, f32[4,4096]{1,0:T(4,128)S(1)}) custom-call(s32[256]{0:T(256)S(1)} %sub.14.refs_0_, s32[1]{0:T(128)} %bitcast.refs_1_.position_ref, f32[8,8192]{1,0:T(8,128)S(1)} %get-tuple-element.25.refs_2_, f32[4,4096]{1,0:T(4,128)S(1)} %collective-permute-done.refs_3_, ...), custom_call_target="tpu_custom_call" | custom-call | flops 6000000000 | bytes 2000000 | tf_op jit(solution)/shard_map/pair_step/pallas_call | solution.py:347
  23.1 1.5 %collective-permute-start.2 = (f32[4,4096]{1,0:T(4,128)S(1)}, f32[4,4096]{1,0:T(4,128)S(1)}, u32[]{:S(2)}, u32[]{:S(2)}) collective-permute-start(f32[4,4096]{1,0:T(4,128)S(1)} %get-tuple-element.32), channel_id=1, source_target_pairs={{0,1},{1,2},{2,3},{3,4},{4,5},{5,6},{6,7},{7,0},{8,9},{9,10},{10,1... | collective-permute-start | bytes 196616 | tf_op jit(solution)/shard_map/ppermute | solution.py:636
  24.7 0.6 collective-permute-start.3
  25.2 0.0 all-to-all-done.point_ref
  25.2 0.0 copy-done.6
  25.2 7.0 %amplitudes.2 = (f32[14,4,8,128]{3,2,1,0:T(8,128)S(1)}, f32[128,128]{1,0:T(8,128)}) custom-call(s32[1]{0:T(128)} %bitcast.refs_1_.position_ref, f32[8,4,256]{2,1,0:T(4,128)S(1)} %all-to-all-done.point_ref, f32[8,2,8,128]{3,2,1,0:T(8,128)S(1)} %copy-done.6), custom_call_target="tpu_custom_call" | custom-call | flops 10000000000 | bytes 1000000 | tf_op jit(solution)/shard_map/amplitudes/pallas_call | solution.py:491
  32.2 9.9 %all-to-all-start.1 = ((f32[128,1,128]{2,1,0:T(1,128)}), f32[128,1,128]{2,1,0:T(1,128)S(1)}, u32[]{:S(2)}, u32[]{:S(2)}) async-start(f32[128,1,128]{2,1,0:T(1,128)} %bitcast.2), calls=%async_computation.1 | async-start | bytes 131072 | tf_op jit(solution)/shard_map/all_to_all | solution.py:640
  42.1 0.0 collective-permute-done.2.refs_3_
  42.1 0.0 collective-permute-done.3.refs_4_
  42.1 7.8 %pair_step.5 = (f32[8,8192]{1,0:T(8,128)S(1)}, f32[4,4096]{1,0:T(4,128)S(1)}, f32[4,4096]{1,0:T(4,128)S(1)}, f32[8,4,256]{2,1,0:T(4,128)}) custom-call(s32[256]{0:T(256)S(1)} %sub.14.refs_0_, s32[1]{0:T(128)} %bitcast.refs_1_.position_ref, f32[8,8192]{1,0:T(8,128)S(1)} %get-tuple-element.31.refs_2_, f32[4,4096]{1,0:T(4,128)S(1)} %collective-permute-done.2.refs_3_, ...), custom_call_target="tpu_custom_call" | custom-call | flops 6000000000 | bytes 2000000 | tf_op jit(solution)/shard_map/pair_step/pallas_call | solution.py:347
  50.0 1.5 %collective-permute-start.4 = (f32[4,4096]{1,0:T(4,128)S(1)}, f32[4,4096]{1,0:T(4,128)S(1)}, u32[]{:S(2)}, u32[]{:S(2)}) collective-permute-start(f32[4,4096]{1,0:T(4,128)S(1)} %get-tuple-element.35), channel_id=1, source_target_pairs={{0,1},{1,2},{2,3},{3,4},{4,5},{5,6},{6,7},{7,0},{8,9},{9,10},{10,1... | collective-permute-start | bytes 196616 | tf_op jit(solution)/shard_map/ppermute | solution.py:636
  51.4 0.6 collective-permute-start.5
  52.0 0.0 all-to-all-done.1
  52.0 6.6 %all-to-all-start.3 = ((f32[8,4,256]{2,1,0:T(4,128)}), f32[8,4,256]{2,1,0:T(4,128)S(1)}, u32[]{:S(2)}, u32[]{:S(2)}) async-start(f32[8,4,256]{2,1,0:T(4,128)} %get-tuple-element.45), calls=%async_computation.3 | async-start | bytes 65536 | tf_op jit(solution)/shard_map/all_to_all | solution.py:640
  58.6 0.0 copy-start.4
  58.6 0.0 copy-start.5
  58.6 0.7 copy-done.4
  59.2 0.0 copy-done.5
  59.3 6.6 %kicks.2 = f32[8,3,256]{2,1,0:T(4,128)} custom-call(s32[1]{0:T(128)} %bitcast.refs_1_.position_ref, f32[8,4,256]{2,1,0:T(4,128)S(1)} %all-to-all-done.point_ref, f32[8,2,8,128]{3,2,1,0:T(8,128)S(1)} %copy-done.6, f32[14,4,8,128]{3,2,1,0:T(8,128)S(1)} %get-tuple-element.38.amp_ref, f32[128,128]{1,0:T(8,128)S(1)} %bitcast.19, f32[1,48]{1,0:T(1,128)S(1)} %bitcast.21, ...), custom_call_target="tpu_custom_call" | custom-call | flops 10000000000 | bytes 1000000 | tf_op jit(solution)/shard_map/kicks/pallas_call | solution.py:607
  65.8 0.0 all-to-all-done.3.point_ref
  65.8 5.7 %all-to-all-start.2 = ((f32[8,3,256]{2,1,0:T(4,128)}), f32[8,3,256]{2,1,0:T(4,128)S(1)}, u32[]{:S(2)}, u32[]{:S(2)}) async-start(f32[8,3,256]{2,1,0:T(4,128)} %kicks.2), calls=%async_computation.2 | async-start | bytes 65536 | tf_op jit(solution)/shard_map/all_to_all | solution.py:640
  71.6 7.0 %amplitudes.3 = (f32[14,4,8,128]{3,2,1,0:T(8,128)S(1)}, f32[128,128]{1,0:T(8,128)}) custom-call(s32[1]{0:T(128)} %bitcast.refs_1_.position_ref, f32[8,4,256]{2,1,0:T(4,128)S(1)} %all-to-all-done.3.point_ref, f32[8,2,8,128]{3,2,1,0:T(8,128)S(1)} %copy-done.6), custom_call_target="tpu_custom_call" | custom-call | flops 10000000000 | bytes 1000000 | tf_op jit(solution)/shard_map/amplitudes/pallas_call | solution.py:491
  78.6 0.0 all-to-all-done.2.refs_7_
  78.6 9.0 %all-to-all-start.4 = ((f32[128,1,128]{2,1,0:T(1,128)}), f32[128,1,128]{2,1,0:T(1,128)S(1)}, u32[]{:S(2)}, u32[]{:S(2)}) async-start(f32[128,1,128]{2,1,0:T(1,128)} %bitcast.8), calls=%async_computation.4 | async-start | bytes 131072 | tf_op jit(solution)/shard_map/all_to_all | solution.py:640
  87.6 0.0 collective-permute-done.4.refs_3_
  87.6 0.0 collective-permute-done.5.refs_4_
  87.6 7.3 %pair_step.6 = (f32[8,8192]{1,0:T(8,128)S(1)}, f32[4,4096]{1,0:T(4,128)S(1)}, f32[4,4096]{1,0:T(4,128)S(1)}) custom-call(s32[256]{0:T(256)S(1)} %sub.14.refs_0_, s32[1]{0:T(128)} %bitcast.refs_1_.position_ref, f32[8,8192]{1,0:T(8,128)S(1)} %get-tuple-element.34.refs_2_, f32[4,4096]{1,0:T(4,128)S(1)} %collective-permute-done.4.refs_3_, ...), custom_call_target="tpu_custom_call" | custom-call | flops 6000000000 | bytes 2000000 | tf_op jit(solution)/shard_map/pair_step/pallas_call | solution.py:347
  94.9 1.5 %collective-permute-start.6 = (f32[4,4096]{1,0:T(4,128)S(1)}, f32[4,4096]{1,0:T(4,128)S(1)}, u32[]{:S(2)}, u32[]{:S(2)}) collective-permute-start(f32[4,4096]{1,0:T(4,128)S(1)} %get-tuple-element.41), channel_id=1, source_target_pairs={{0,1},{1,2},{2,3},{3,4},{4,5},{5,6},{6,7},{7,0},{8,9},{9,10},{10,1... | collective-permute-start | bytes 196616 | tf_op jit(solution)/shard_map/ppermute | solution.py:636
  96.4 0.6 collective-permute-start.7
  97.0 0.0 all-to-all-done.4
  97.0 6.6 %kicks.3 = f32[8,3,256]{2,1,0:T(4,128)} custom-call(s32[1]{0:T(128)} %bitcast.refs_1_.position_ref, f32[8,4,256]{2,1,0:T(4,128)S(1)} %all-to-all-done.3.point_ref, f32[8,2,8,128]{3,2,1,0:T(8,128)S(1)} %copy-done.6, f32[14,4,8,128]{3,2,1,0:T(8,128)S(1)} %get-tuple-element.46.amp_ref, f32[128,128]{1,0:T(8,128)S(1)} %bitcast.20, f32[1,48]{1,0:T(1,128)S(1)} %bitcast.22, ...), custom_call_target="tpu_custom_call" | custom-call | flops 10000000000 | bytes 1000000 | tf_op jit(solution)/shard_map/kicks/pallas_call | solution.py:607
  103.6 6.6 %all-to-all-start.5 = ((f32[8,3,256]{2,1,0:T(4,128)}), f32[8,3,256]{2,1,0:T(4,128)S(1)}, u32[]{:S(2)}, u32[]{:S(2)}) async-start(f32[8,3,256]{2,1,0:T(4,128)} %kicks.3), calls=%async_computation.5 | async-start | bytes 65536 | tf_op jit(solution)/shard_map/all_to_all | solution.py:640
  110.2 0.0 collective-permute-done.6.refs_3_
  110.2 0.0 collective-permute-done.7.refs_4_
  110.2 6.9 %pair_step.7 = (f32[3,8192]{1,0:T(4,128)S(1)}, f32[3,8192]{1,0:T(4,128)S(1)}) custom-call(s32[256]{0:T(256)S(1)} %sub.14.refs_0_, s32[1]{0:T(128)} %bitcast.refs_1_.position_ref, f32[8,8192]{1,0:T(8,128)S(1)} %get-tuple-element.40.refs_2_, f32[4,4096]{1,0:T(4,128)S(1)} %collective-permute-done.6.refs_3_, f32[4,4096]{1,0:T(4,128)S(1)} %collective-permute-done.7.refs_4_), custom_call_target="tpu_custom_call" | custom-call | flops 6000000000 | bytes 2000000 | tf_op jit(solution)/shard_map/pair_step/pallas_call | solution.py:347
  117.2 0.7 copy.16
  117.9 0.0 all-to-all-done.5.kick_ref
  117.9 0.4 finish.1
  118.4 0.7 copy.17
  (3 shorter events, 0.0 us)
Async XLA Ops:
  0.6 1.1 copy-start.1
  0.6 1.1 copy-start
  0.7 1.1 copy-start.3
  1.8 0.7 copy-start.2
  2.4 3.1 %copy-start.7 = (s32[1,4,64,4]{2,3,1,0:T(4,128)S(1)}, s32[1,4,64,4]{2,3,1,0:T(4,128)}, u32[]{:S(2)}) copy-start(s32[1,4,64,4]{2,3,1,0:T(4,128)} %param.14) | copy-start | bytes 12292
  3.5 4.3 %collective-permute-start = (f32[4,4096]{1,0:T(4,128)S(1)}, f32[4,4096]{1,0:T(4,128)S(1)}, u32[]{:S(2)}, u32[]{:S(2)}) collective-permute-start(f32[4,4096]{1,0:T(4,128)S(1)} %get-tuple-element.27), channel_id=1, source_target_pairs={{0,1},{1,2},{2,3},{3,4},{4,5},{5,6},{6,7},{7,0},{8,9},{9,10},{10,1... | collective-permute-start | bytes 196616 | tf_op jit(solution)/shard_map/ppermute | solution.py:636
  5.0 4.3 %collective-permute-start.1 = (f32[4,4096]{1,0:T(4,128)S(1)}, f32[4,4096]{1,0:T(4,128)S(1)}, u32[]{:S(2)}, u32[]{:S(2)}) collective-permute-start(f32[4,4096]{1,0:T(4,128)S(1)} %get-tuple-element.28), channel_id=1, source_target_pairs={{1,0},{2,1},{3,2},{4,3},{5,4},{6,5},{7,6},{0,7},{9,8},{10,9},{11,1... | collective-permute-start | bytes 196616 | tf_op jit(solution)/shard_map/ppermute | solution.py:636
  9.3 15.9 %all-to-all-start = ((f32[8,4,256]{2,1,0:T(4,128)}), f32[8,4,256]{2,1,0:T(4,128)S(1)}, u32[]{:S(2)}, u32[]{:S(2)}) async-start(f32[8,4,256]{2,1,0:T(4,128)} %get-tuple-element.37), calls=%async_computation | async-start | bytes 65536 | tf_op jit(solution)/shard_map/all_to_all | solution.py:640
  16.2 9.1 %copy-start.6 = (f32[8,2,8,128]{3,2,1,0:T(8,128)S(1)}, f32[8,2,8,128]{3,2,1,0:T(8,128)}, u32[]{:S(2)}) copy-start(f32[8,2,8,128]{3,2,1,0:T(8,128)} %constant.12.clone.dir_ref) | copy-start | bytes 196612
  23.1 19.0 %collective-permute-start.2 = (f32[4,4096]{1,0:T(4,128)S(1)}, f32[4,4096]{1,0:T(4,128)S(1)}, u32[]{:S(2)}, u32[]{:S(2)}) collective-permute-start(f32[4,4096]{1,0:T(4,128)S(1)} %get-tuple-element.32), channel_id=1, source_target_pairs={{0,1},{1,2},{2,3},{3,4},{4,5},{5,6},{6,7},{7,0},{8,9},{9,10},{10,1... | collective-permute-start | bytes 196616 | tf_op jit(solution)/shard_map/ppermute | solution.py:636
  24.7 17.5 %collective-permute-start.3 = (f32[4,4096]{1,0:T(4,128)S(1)}, f32[4,4096]{1,0:T(4,128)S(1)}, u32[]{:S(2)}, u32[]{:S(2)}) collective-permute-start(f32[4,4096]{1,0:T(4,128)S(1)} %get-tuple-element.33), channel_id=1, source_target_pairs={{1,0},{2,1},{3,2},{4,3},{5,4},{6,5},{7,6},{0,7},{9,8},{10,9},{11,1... | collective-permute-start | bytes 196616 | tf_op jit(solution)/shard_map/ppermute | solution.py:636
  32.2 19.8 %all-to-all-start.1 = ((f32[128,1,128]{2,1,0:T(1,128)}), f32[128,1,128]{2,1,0:T(1,128)S(1)}, u32[]{:S(2)}, u32[]{:S(2)}) async-start(f32[128,1,128]{2,1,0:T(1,128)} %bitcast.2), calls=%async_computation.1 | async-start | bytes 131072 | tf_op jit(solution)/shard_map/all_to_all | solution.py:640
  50.0 37.6 %collective-permute-start.4 = (f32[4,4096]{1,0:T(4,128)S(1)}, f32[4,4096]{1,0:T(4,128)S(1)}, u32[]{:S(2)}, u32[]{:S(2)}) collective-permute-start(f32[4,4096]{1,0:T(4,128)S(1)} %get-tuple-element.35), channel_id=1, source_target_pairs={{0,1},{1,2},{2,3},{3,4},{4,5},{5,6},{6,7},{7,0},{8,9},{9,10},{10,1... | collective-permute-start | bytes 196616 | tf_op jit(solution)/shard_map/ppermute | solution.py:636
  51.4 36.1 %collective-permute-start.5 = (f32[4,4096]{1,0:T(4,128)S(1)}, f32[4,4096]{1,0:T(4,128)S(1)}, u32[]{:S(2)}, u32[]{:S(2)}) collective-permute-start(f32[4,4096]{1,0:T(4,128)S(1)} %get-tuple-element.36), channel_id=1, source_target_pairs={{1,0},{2,1},{3,2},{4,3},{5,4},{6,5},{7,6},{0,7},{9,8},{10,9},{11,1... | collective-permute-start | bytes 196616 | tf_op jit(solution)/shard_map/ppermute | solution.py:636
  52.0 13.8 %all-to-all-start.3 = ((f32[8,4,256]{2,1,0:T(4,128)}), f32[8,4,256]{2,1,0:T(4,128)S(1)}, u32[]{:S(2)}, u32[]{:S(2)}) async-start(f32[8,4,256]{2,1,0:T(4,128)} %get-tuple-element.45), calls=%async_computation.3 | async-start | bytes 65536 | tf_op jit(solution)/shard_map/all_to_all | solution.py:640
  58.6 0.7 copy-start.4
  58.6 0.7 copy-start.5
  65.8 12.7 %all-to-all-start.2 = ((f32[8,3,256]{2,1,0:T(4,128)}), f32[8,3,256]{2,1,0:T(4,128)S(1)}, u32[]{:S(2)}, u32[]{:S(2)}) async-start(f32[8,3,256]{2,1,0:T(4,128)} %kicks.2), calls=%async_computation.2 | async-start | bytes 65536 | tf_op jit(solution)/shard_map/all_to_all | solution.py:640
  78.6 18.4 %all-to-all-start.4 = ((f32[128,1,128]{2,1,0:T(1,128)}), f32[128,1,128]{2,1,0:T(1,128)S(1)}, u32[]{:S(2)}, u32[]{:S(2)}) async-start(f32[128,1,128]{2,1,0:T(1,128)} %bitcast.8), calls=%async_computation.4 | async-start | bytes 131072 | tf_op jit(solution)/shard_map/all_to_all | solution.py:640
  94.9 15.3 %collective-permute-start.6 = (f32[4,4096]{1,0:T(4,128)S(1)}, f32[4,4096]{1,0:T(4,128)S(1)}, u32[]{:S(2)}, u32[]{:S(2)}) collective-permute-start(f32[4,4096]{1,0:T(4,128)S(1)} %get-tuple-element.41), channel_id=1, source_target_pairs={{0,1},{1,2},{2,3},{3,4},{4,5},{5,6},{6,7},{7,0},{8,9},{9,10},{10,1... | collective-permute-start | bytes 196616 | tf_op jit(solution)/shard_map/ppermute | solution.py:636
  96.4 13.8 %collective-permute-start.7 = (f32[4,4096]{1,0:T(4,128)S(1)}, f32[4,4096]{1,0:T(4,128)S(1)}, u32[]{:S(2)}, u32[]{:S(2)}) collective-permute-start(f32[4,4096]{1,0:T(4,128)S(1)} %get-tuple-element.42), channel_id=1, source_target_pairs={{1,0},{2,1},{3,2},{4,3},{5,4},{6,5},{7,6},{0,7},{9,8},{10,9},{11,1... | collective-permute-start | bytes 196616 | tf_op jit(solution)/shard_map/ppermute | solution.py:636
  103.6 14.4 %all-to-all-start.5 = ((f32[8,3,256]{2,1,0:T(4,128)}), f32[8,3,256]{2,1,0:T(4,128)S(1)}, u32[]{:S(2)}, u32[]{:S(2)}) async-start(f32[8,3,256]{2,1,0:T(4,128)} %kicks.3), calls=%async_computation.5 | async-start | bytes 65536 | tf_op jit(solution)/shard_map/all_to_all | solution.py:640
where the time goes:
time: 120 us; the launch traced here: 119 us
  Pallas kernels  57.7 us (48%)
  starting transfers between devices  52.9 us (44%)
  local copies, waits for them, and re-layouts  4 us (3%)
  waiting for transfers between devices  3.73 us (3%)
    all_to_all x6, starting transfers between devices, to_all(): return lax.all_to_all(value, axes, 0, 0, tiled=True)  44.7 us
    pallas_call x4, Pallas kernels, pair_step(): pl.pallas_call(functools.partial(pair_kernel, step, kicked, gathers, last...  29 us
    pallas_call x2, Pallas kernels, amplitudes(): pl.pallas_call(amplitude_kernel, grid_spec=pltpu.PrefetchScalarGridSpec(n...  14 us
    pallas_call x2, Pallas kernels, kicks(): pl.pallas_call(kick_kernel, grid_spec=pltpu.PrefetchScalarGridSpec(num_sc...  13.2 us
    ppermute x8, starting transfers between devices, exchange(): return (lax.ppermute(tail, 'sp', right), lax.ppermute(head, 'sp', left))  8.24 us
    unnamed x19, local copies, waits for them, and re-layouts  3.92 us
    ppermute x8, waiting for transfers between devices, exchange(): return (lax.ppermute(tail, 'sp', right), lax.ppermute(head, 'sp', left))  3.71 us
  transfers between devices with their start and end apart: 14, of which 2 were waited for; matrix products, arithmetic and copies ran while one was open for 1% of the time, Pallas kernels for 47%

commit v1 on v0

--- a/solution.py
+++ b/solution.py
@@ -28,9 +28,10 @@
 PARTS = 8
 REPLICAS = 16
 DIR_PART = M // PARTS
-STEP_GROUPS = 7
+GROUPS = -(-DIR_PART // 8)
 STEPS = 2
-GROUPS = STEPS * STEP_GROUPS
+FULL = GROUPS // STEPS
+SLOTS = FULL + 1
 SIDE = 4
 CENTERS = NQ // (2 * SIDE)
 LANE_GROUPS = PARTS * SOL // 128
@@ -55,10 +56,13 @@
     rows = np.stack([radius * np.cos(azimuth), radius * np.sin(azimuth), height], axis=-1) * TURN
     padded = np.zeros((PARTS, GROUPS * 8, 3), np.float32)
     padded[:, :DIR_PART] = rows.reshape(PARTS, DIR_PART, 3)
+    padded = padded.reshape(PARTS, GROUPS, 8, 3)
     table = np.zeros((PARTS, STEPS, 8, 128), np.float32)
-    for c in range(3):
-        part = padded[:, :, c].reshape(PARTS, STEPS, STEP_GROUPS, 8)
-        table[:, :, :, 16 * c : 16 * c + STEP_GROUPS] = np.swapaxes(part, 2, 3)
+    for turn in range(STEPS):
+        for slot in range(SLOTS):
+            group = turn * FULL + slot if slot < FULL else GROUPS - 1
+            for c in range(3):
+                table[:, turn, :, 16 * c + slot] = padded[:, group, :, c]
     return table
 
 
@@ -411,15 +415,14 @@
     lane = lax.broadcasted_iota(jnp.int32, (8, 128), 1)
 
     turn = pl.program_id(0)
-    for group in range(STEP_GROUPS):
-        u = group_directions(dir_ref, group)
+    for slot in range(SLOTS):
+        u = group_directions(dir_ref, slot)
         total = None
-        for at in range(LANE_GROUPS // CHUNK):
+        for at in chunks_of(slot):
             left = []
             right = []
             for n in range(CHUNK):
-                j = at * CHUNK + n
-                turns, weight = group_turns(u, point_ref, j // 2, j % 2)
+                turns, weight = group_turns(u, point_ref, part_of(turn, slot, at, n), n % 2)
                 powers, step, start = unit_powers(turns)
                 high, low = term_rows(powers)
                 right.append(jnp.concatenate(high + low, axis=0))
@@ -442,7 +445,7 @@
                 preferred_element_type=F32,
             )
             total = part if total is None else total + part
-        total_ref[turn * STEP_GROUPS + group] = total[0 : 16 * CENTERS] + total[16 * CENTERS :]
+        total_ref[turn * SLOTS + slot] = total[0 : 16 * CENTERS] + total[16 * CENTERS :]
 
     @pl.when(turn == STEPS - 1)
     def _():
@@ -450,11 +453,15 @@
         front = lane < 8 * SIDE
         squares = [jnp.zeros((8, 128), F32)] * 2
         for g in range(GROUPS):
+            if g < GROUPS - 1:
+                sums = total_ref[g // FULL * SLOTS + g % FULL]
+            else:
+                sums = total_ref[FULL] + total_ref[SLOTS + FULL]
             real = jnp.zeros((8, 128), F32)
             imag = real
             for k in range(CENTERS):
-                c = jnp.sum(jnp.where(own, total_ref[g, 16 * k : 16 * k + 8], 0.0), axis=0, keepdims=True)
-                s = jnp.sum(jnp.where(own, total_ref[g, 16 * k + 8 : 16 * k + 16], 0.0), axis=0, keepdims=True)
+                c = jnp.sum(jnp.where(own, sums[16 * k : 16 * k + 8], 0.0), axis=0, keepdims=True)
+                s = jnp.sum(jnp.where(own, sums[16 * k + 8 : 16 * k + 16], 0.0), axis=0, keepdims=True)
                 real = jnp.where(row == k, c, real)
                 imag = jnp.where(row == k, s, imag)
             real = (real + pltpu.roll(real, 64, axis=1)) * NORM
@@ -479,6 +486,15 @@
         inten_ref[...] = jnp.broadcast_to(spread, inten_ref.shape)
 
 
+def chunks_of(slot):
+    return range(LANE_GROUPS // CHUNK if slot < FULL else LANE_GROUPS // CHUNK // STEPS)
+
+
+def part_of(turn, slot, at, n):
+    part = (at * CHUNK + n) // 2
+    return part if slot < FULL else turn * (PARTS // STEPS) + part
+
+
 def point_spec():
     return pl.BlockSpec((PARTS, 4, SOL), lambda g, p: (0, 0, 0))
 
@@ -498,7 +514,7 @@
                 pl.BlockSpec((GROUPS, 4, 8, 128), lambda g, p: (0, 0, 0, 0)),
                 pl.BlockSpec((PARTS * REPLICAS, 128), lambda g, p: (0, 0)),
             ],
-            scratch_shapes=[pltpu.VMEM((GROUPS, 16 * CENTERS, 128), F32)],
+            scratch_shapes=[pltpu.VMEM((STEPS * SLOTS, 16 * CENTERS, 128), F32)],
         ),
         out_shape=[
             jax.ShapeDtypeStruct((GROUPS, 4, 8, 128), F32),
@@ -551,21 +567,23 @@
                 coef_ref[g, at, 128:256] = last
 
     kicked = [[None] * 3 for _ in range(LANE_GROUPS)]
+    halved = [[None] * 3 for _ in range(LANE_GROUPS // STEPS)]
     turn = pl.program_id(0)
-    for group in range(STEP_GROUPS):
-        u = group_directions(dir_ref, group)
-
-        for at in range(LANE_GROUPS // CHUNK):
+    for slot in range(SLOTS):
+        u = group_directions(dir_ref, slot)
+        held = kicked if slot < FULL else halved
+        group = turn * FULL + slot if slot < FULL else GROUPS - 1
+
+        for at in chunks_of(slot):
             state = []
             columns = []
             for n in range(CHUNK):
-                j = at * CHUNK + n
-                turns, _ = group_turns(u, point_ref, j // 2, j % 2)
+                turns, _ = group_turns(u, point_ref, part_of(turn, slot, at, n), n % 2)
                 powers, step, start = unit_powers(turns)
                 high, low = term_rows(powers)
                 columns.append(jnp.concatenate(high + low + high, axis=0))
                 state.append([step, start, step[0] + step[0]])
-            terms = jnp.dot(coef_ref[turn * STEP_GROUPS + group, :, 0:192], jnp.concatenate(columns, axis=1), preferred_element_type=F32)
+            terms = jnp.dot(coef_ref[group, :, 0:192], jnp.concatenate(columns, axis=1), preferred_element_type=F32)
             for n in range(CHUNK):
                 step, start, twice = state[n]
                 lanes = slice(n * 128, n * 128 + 128)
@@ -585,14 +603,18 @@
                 slope = real * start[0] - imag * start[1]
                 for c in range(3):
                     value = u[c] * slope
-                    old = kicked[at * CHUNK + n][c]
-                    kicked[at * CHUNK + n][c] = value if old is None else old + value
+                    old = held[at * CHUNK + n][c]
+                    held[at * CHUNK + n][c] = value if old is None else old + value
 
     @pl.when(turn == 0)
     def _():
         for j in range(LANE_GROUPS):
             for c in range(3):
                 acc_ref[3 * j + c] = kicked[j][c]
+
+    for j in range(LANE_GROUPS // STEPS):
+        for c in range(3):
+            acc_ref[3 * (turn * (LANE_GROUPS // STEPS) + j) + c] += halved[j][c]
 
     @pl.when(turn == STEPS - 1)
     def _():

time: 120 us -> 118 us (0.983)
  Pallas kernels: 57.7 us -> 56.2 us
where the time goes in v1:
time: 118 us
  Pallas kernels  56.2 us (48%)
  starting transfers between devices  52.9 us (45%)
  local copies, waits for them, and re-layouts  4 us (3%)
  waiting for transfers between devices  3.73 us (3%)
    all_to_all x6, starting transfers between devices, to_all(): return lax.all_to_all(value, axes, 0, 0, tiled=True)  44.6 us
    pallas_call x4, Pallas kernels, pair_step(): pl.pallas_call(functools.partial(pair_kernel, step, kicked, gathers, last...  29 us
    pallas_call x2, Pallas kernels, amplitudes(): pl.pallas_call(amplitude_kernel, grid_spec=pltpu.PrefetchScalarGridSpec(n...  13.2 us
    pallas_call x2, Pallas kernels, kicks(): pl.pallas_call(kick_kernel, grid_spec=pltpu.PrefetchScalarGridSpec(num_sc...  12.4 us
    ppermute x8, starting transfers between devices, exchange(): return (lax.ppermute(tail, 'sp', right), lax.ppermute(head, 'sp', left))  8.24 us
    unnamed x19, local copies, waits for them, and re-layouts  3.92 us
    ppermute x8, waiting for transfers between devices, exchange(): return (lax.ppermute(tail, 'sp', right), lax.ppermute(head, 'sp', left))  3.71 us
  transfers between devices with their start and end apart: 14, of which 2 were waited for; matrix products, arithmetic and copies ran while one was open for 1% of the time, Pallas kernels for 47%

profile of v1, /device:TPU:8, one launch (start us, length us, event | category | flops | bytes accessed | tf_op | source)
XLA Modules:
  0.0 117.6 jit_solution(10541829574809540009)
XLA Ops:
  0.6 0.0 copy-start.1
  0.6 0.0 copy-start
  0.7 0.0 copy-start.3
  0.7 1.1 copy_bitcast_fusion
  1.8 0.0 copy-start.2
  1.8 0.0 copy-done.1
  1.8 0.0 copy-done
  1.8 0.0 copy-done.3
  1.8 0.6 copy-done.2
  2.4 0.0 copy-start.7
  2.4 1.0 pack.1
  3.5 1.6 %collective-permute-start = (f32[4,4096]{1,0:T(4,128)S(1)}, f32[4,4096]{1,0:T(4,128)S(1)}, u32[]{:S(2)}, u32[]{:S(2)}) collective-permute-start(f32[4,4096]{1,0:T(4,128)S(1)} %get-tuple-element.27), channel_id=1, source_target_pairs={{0,1},{1,2},{2,3},{3,4},{4,5},{5,6},{6,7},{7,0},{8,9},{9,10},{10,1... | collective-permute-start | bytes 196616 | tf_op jit(solution)/shard_map/ppermute | solution.py:658
  5.0 0.4 collective-permute-start.1
  5.5 0.0 copy-done.7
  5.5 0.1 sub.14.refs_0_
  5.6 2.1 %collective-permute-done.refs_3_ = f32[4,4096]{1,0:T(4,128)S(1)} collective-permute-done((f32[4,4096]{1,0:T(4,128)S(1)}, f32[4,4096]{1,0:T(4,128)S(1)}, u32[]{:S(2)}, u32[]{:S(2)}) %collective-permute-start) | collective-permute-done | bytes 65568 | tf_op jit(solution)/shard_map/ppermute | solution.py:658
  7.7 1.6 %collective-permute-done.1.refs_4_ = f32[4,4096]{1,0:T(4,128)S(1)} collective-permute-done((f32[4,4096]{1,0:T(4,128)S(1)}, f32[4,4096]{1,0:T(4,128)S(1)}, u32[]{:S(2)}, u32[]{:S(2)}) %collective-permute-start.1) | collective-permute-done | bytes 65568 | tf_op jit(solution)/shard_map/ppermute | solution.py:658
  9.3 6.8 %all-to-all-start = ((f32[8,4,256]{2,1,0:T(4,128)}), f32[8,4,256]{2,1,0:T(4,128)S(1)}, u32[]{:S(2)}, u32[]{:S(2)}) async-start(f32[8,4,256]{2,1,0:T(4,128)} %get-tuple-element.37), calls=%async_computation | async-start | bytes 65536 | tf_op jit(solution)/shard_map/all_to_all | solution.py:662
  16.2 0.0 copy-start.6
  16.2 7.0 %pair_step.4 = (f32[8,8192]{1,0:T(8,128)S(1)}, f32[4,4096]{1,0:T(4,128)S(1)}, f32[4,4096]{1,0:T(4,128)S(1)}) custom-call(s32[256]{0:T(256)S(1)} %sub.14.refs_0_, s32[1]{0:T(128)} %bitcast.refs_1_.position_ref, f32[8,8192]{1,0:T(8,128)S(1)} %get-tuple-element.25.refs_2_, f32[4,4096]{1,0:T(4,128)S(1)} %collective-permute-done.refs_3_, ...), custom_call_target="tpu_custom_call" | custom-call | flops 6000000000 | bytes 2000000 | tf_op jit(solution)/shard_map/pair_step/pallas_call | solution.py:351
  23.1 1.5 %collective-permute-start.2 = (f32[4,4096]{1,0:T(4,128)S(1)}, f32[4,4096]{1,0:T(4,128)S(1)}, u32[]{:S(2)}, u32[]{:S(2)}) collective-permute-start(f32[4,4096]{1,0:T(4,128)S(1)} %get-tuple-element.32), channel_id=1, source_target_pairs={{0,1},{1,2},{2,3},{3,4},{4,5},{5,6},{6,7},{7,0},{8,9},{9,10},{10,1... | collective-permute-start | bytes 196616 | tf_op jit(solution)/shard_map/ppermute | solution.py:658
  24.7 0.6 collective-permute-start.3
  25.2 0.0 all-to-all-done.point_ref
  25.2 0.0 copy-done.6
  25.2 6.6 %amplitudes.2 = (f32[13,4,8,128]{3,2,1,0:T(8,128)S(1)}, f32[128,128]{1,0:T(8,128)}) custom-call(s32[1]{0:T(128)} %bitcast.refs_1_.position_ref, f32[8,4,256]{2,1,0:T(4,128)S(1)} %all-to-all-done.point_ref, f32[8,2,8,128]{3,2,1,0:T(8,128)S(1)} %copy-done.6), custom_call_target="tpu_custom_call" | custom-call | flops 10000000000 | bytes 1000000 | tf_op jit(solution)/shard_map/amplitudes/pallas_call | solution.py:507
  31.9 9.9 %all-to-all-start.1 = ((f32[128,1,128]{2,1,0:T(1,128)}), f32[128,1,128]{2,1,0:T(1,128)S(1)}, u32[]{:S(2)}, u32[]{:S(2)}) async-start(f32[128,1,128]{2,1,0:T(1,128)} %bitcast.2), calls=%async_computation.1 | async-start | bytes 131072 | tf_op jit(solution)/shard_map/all_to_all | solution.py:662
  41.8 0.0 collective-permute-done.2.refs_3_
  41.8 0.0 collective-permute-done.3.refs_4_
  41.8 7.8 %pair_step.5 = (f32[8,8192]{1,0:T(8,128)S(1)}, f32[4,4096]{1,0:T(4,128)S(1)}, f32[4,4096]{1,0:T(4,128)S(1)}, f32[8,4,256]{2,1,0:T(4,128)}) custom-call(s32[256]{0:T(256)S(1)} %sub.14.refs_0_, s32[1]{0:T(128)} %bitcast.refs_1_.position_ref, f32[8,8192]{1,0:T(8,128)S(1)} %get-tuple-element.31.refs_2_, f32[4,4096]{1,0:T(4,128)S(1)} %collective-permute-done.2.refs_3_, ...), custom_call_target="tpu_custom_call" | custom-call | flops 6000000000 | bytes 2000000 | tf_op jit(solution)/shard_map/pair_step/pallas_call | solution.py:351
  49.6 1.5 %collective-permute-start.4 = (f32[4,4096]{1,0:T(4,128)S(1)}, f32[4,4096]{1,0:T(4,128)S(1)}, u32[]{:S(2)}, u32[]{:S(2)}) collective-permute-start(f32[4,4096]{1,0:T(4,128)S(1)} %get-tuple-element.35), channel_id=1, source_target_pairs={{0,1},{1,2},{2,3},{3,4},{4,5},{5,6},{6,7},{7,0},{8,9},{9,10},{10,1... | collective-permute-start | bytes 196616 | tf_op jit(solution)/shard_map/ppermute | solution.py:658
  51.1 0.6 collective-permute-start.5
  51.6 0.0 all-to-all-done.1
  51.6 6.6 %all-to-all-start.3 = ((f32[8,4,256]{2,1,0:T(4,128)}), f32[8,4,256]{2,1,0:T(4,128)S(1)}, u32[]{:S(2)}, u32[]{:S(2)}) async-start(f32[8,4,256]{2,1,0:T(4,128)} %get-tuple-element.45), calls=%async_computation.3 | async-start | bytes 65536 | tf_op jit(solution)/shard_map/all_to_all | solution.py:662
  58.2 0.0 copy-start.4
  58.2 0.0 copy-start.5
  58.2 0.7 copy-done.4
  58.9 0.0 copy-done.5
  58.9 6.2 %kicks.2 = f32[8,3,256]{2,1,0:T(4,128)} custom-call(s32[1]{0:T(128)} %bitcast.refs_1_.position_ref, f32[8,4,256]{2,1,0:T(4,128)S(1)} %all-to-all-done.point_ref, f32[8,2,8,128]{3,2,1,0:T(8,128)S(1)} %copy-done.6, f32[13,4,8,128]{3,2,1,0:T(8,128)S(1)} %get-tuple-element.38.amp_ref, f32[128,128]{1,0:T(8,128)S(1)} %bitcast.19, f32[1,48]{1,0:T(1,128)S(1)} %bitcast.21, ...), custom_call_target="tpu_custom_call" | custom-call | flops 10000000000 | bytes 1000000 | tf_op jit(solution)/shard_map/kicks/pallas_call | solution.py:629
  65.1 0.0 all-to-all-done.3.point_ref
  65.1 5.7 %all-to-all-start.2 = ((f32[8,3,256]{2,1,0:T(4,128)}), f32[8,3,256]{2,1,0:T(4,128)S(1)}, u32[]{:S(2)}, u32[]{:S(2)}) async-start(f32[8,3,256]{2,1,0:T(4,128)} %kicks.2), calls=%async_computation.2 | async-start | bytes 65536 | tf_op jit(solution)/shard_map/all_to_all | solution.py:662
  70.8 6.6 %amplitudes.3 = (f32[13,4,8,128]{3,2,1,0:T(8,128)S(1)}, f32[128,128]{1,0:T(8,128)}) custom-call(s32[1]{0:T(128)} %bitcast.refs_1_.position_ref, f32[8,4,256]{2,1,0:T(4,128)S(1)} %all-to-all-done.3.point_ref, f32[8,2,8,128]{3,2,1,0:T(8,128)S(1)} %copy-done.6), custom_call_target="tpu_custom_call" | custom-call | flops 10000000000 | bytes 1000000 | tf_op jit(solution)/shard_map/amplitudes/pallas_call | solution.py:507
  77.5 0.0 all-to-all-done.2.refs_7_
  77.5 9.0 %all-to-all-start.4 = ((f32[128,1,128]{2,1,0:T(1,128)}), f32[128,1,128]{2,1,0:T(1,128)S(1)}, u32[]{:S(2)}, u32[]{:S(2)}) async-start(f32[128,1,128]{2,1,0:T(1,128)} %bitcast.8), calls=%async_computation.4 | async-start | bytes 131072 | tf_op jit(solution)/shard_map/all_to_all | solution.py:662
  86.4 0.0 collective-permute-done.4.refs_3_
  86.4 0.0 collective-permute-done.5.refs_4_
  86.4 7.3 %pair_step.6 = (f32[8,8192]{1,0:T(8,128)S(1)}, f32[4,4096]{1,0:T(4,128)S(1)}, f32[4,4096]{1,0:T(4,128)S(1)}) custom-call(s32[256]{0:T(256)S(1)} %sub.14.refs_0_, s32[1]{0:T(128)} %bitcast.refs_1_.position_ref, f32[8,8192]{1,0:T(8,128)S(1)} %get-tuple-element.34.refs_2_, f32[4,4096]{1,0:T(4,128)S(1)} %collective-permute-done.4.refs_3_, ...), custom_call_target="tpu_custom_call" | custom-call | flops 6000000000 | bytes 2000000 | tf_op jit(solution)/shard_map/pair_step/pallas_call | solution.py:351
  93.8 1.5 %collective-permute-start.6 = (f32[4,4096]{1,0:T(4,128)S(1)}, f32[4,4096]{1,0:T(4,128)S(1)}, u32[]{:S(2)}, u32[]{:S(2)}) collective-permute-start(f32[4,4096]{1,0:T(4,128)S(1)} %get-tuple-element.41), channel_id=1, source_target_pairs={{0,1},{1,2},{2,3},{3,4},{4,5},{5,6},{6,7},{7,0},{8,9},{9,10},{10,1... | collective-permute-start | bytes 196616 | tf_op jit(solution)/shard_map/ppermute | solution.py:658
  95.3 0.6 collective-permute-start.7
  95.8 0.0 all-to-all-done.4
  95.9 6.2 %kicks.3 = f32[8,3,256]{2,1,0:T(4,128)} custom-call(s32[1]{0:T(128)} %bitcast.refs_1_.position_ref, f32[8,4,256]{2,1,0:T(4,128)S(1)} %all-to-all-done.3.point_ref, f32[8,2,8,128]{3,2,1,0:T(8,128)S(1)} %copy-done.6, f32[13,4,8,128]{3,2,1,0:T(8,128)S(1)} %get-tuple-element.46.amp_ref, f32[128,128]{1,0:T(8,128)S(1)} %bitcast.20, f32[1,48]{1,0:T(1,128)S(1)} %bitcast.22, ...), custom_call_target="tpu_custom_call" | custom-call | flops 10000000000 | bytes 1000000 | tf_op jit(solution)/shard_map/kicks/pallas_call | solution.py:629
  102.1 6.6 %all-to-all-start.5 = ((f32[8,3,256]{2,1,0:T(4,128)}), f32[8,3,256]{2,1,0:T(4,128)S(1)}, u32[]{:S(2)}, u32[]{:S(2)}) async-start(f32[8,3,256]{2,1,0:T(4,128)} %kicks.3), calls=%async_computation.5 | async-start | bytes 65536 | tf_op jit(solution)/shard_map/all_to_all | solution.py:662
  108.7 0.0 collective-permute-done.6.refs_3_
  108.7 0.0 collective-permute-done.7.refs_4_
  108.7 6.9 %pair_step.7 = (f32[3,8192]{1,0:T(4,128)S(1)}, f32[3,8192]{1,0:T(4,128)S(1)}) custom-call(s32[256]{0:T(256)S(1)} %sub.14.refs_0_, s32[1]{0:T(128)} %bitcast.refs_1_.position_ref, f32[8,8192]{1,0:T(8,128)S(1)} %get-tuple-element.40.refs_2_, f32[4,4096]{1,0:T(4,128)S(1)} %collective-permute-done.6.refs_3_, f32[4,4096]{1,0:T(4,128)S(1)} %collective-permute-done.7.refs_4_), custom_call_target="tpu_custom_call" | custom-call | flops 6000000000 | bytes 2000000 | tf_op jit(solution)/shard_map/pair_step/pallas_call | solution.py:351
  115.7 0.7 copy.16
  116.4 0.0 all-to-all-done.5.kick_ref
  116.4 0.4 finish.1
  116.9 0.7 copy.17
  (3 shorter events, 0.0 us)
Async XLA Ops:
  0.6 1.1 copy-start.1
  0.6 1.1 copy-start
  0.7 1.1 copy-start.3
  1.8 0.7 copy-start.2
  2.4 3.1 %copy-start.7 = (s32[1,4,64,4]{2,3,1,0:T(4,128)S(1)}, s32[1,4,64,4]{2,3,1,0:T(4,128)}, u32[]{:S(2)}) copy-start(s32[1,4,64,4]{2,3,1,0:T(4,128)} %param.14) | copy-start | bytes 12292
  3.5 4.3 %collective-permute-start = (f32[4,4096]{1,0:T(4,128)S(1)}, f32[4,4096]{1,0:T(4,128)S(1)}, u32[]{:S(2)}, u32[]{:S(2)}) collective-permute-start(f32[4,4096]{1,0:T(4,128)S(1)} %get-tuple-element.27), channel_id=1, source_target_pairs={{0,1},{1,2},{2,3},{3,4},{4,5},{5,6},{6,7},{7,0},{8,9},{9,10},{10,1... | collective-permute-start | bytes 196616 | tf_op jit(solution)/shard_map/ppermute | solution.py:658
  5.0 4.3 %collective-permute-start.1 = (f32[4,4096]{1,0:T(4,128)S(1)}, f32[4,4096]{1,0:T(4,128)S(1)}, u32[]{:S(2)}, u32[]{:S(2)}) collective-permute-start(f32[4,4096]{1,0:T(4,128)S(1)} %get-tuple-element.28), channel_id=1, source_target_pairs={{1,0},{2,1},{3,2},{4,3},{5,4},{6,5},{7,6},{0,7},{9,8},{10,9},{11,1... | collective-permute-start | bytes 196616 | tf_op jit(solution)/shard_map/ppermute | solution.py:658
  9.3 15.9 %all-to-all-start = ((f32[8,4,256]{2,1,0:T(4,128)}), f32[8,4,256]{2,1,0:T(4,128)S(1)}, u32[]{:S(2)}, u32[]{:S(2)}) async-start(f32[8,4,256]{2,1,0:T(4,128)} %get-tuple-element.37), calls=%async_computation | async-start | bytes 65536 | tf_op jit(solution)/shard_map/all_to_all | solution.py:662
  16.2 9.1 %copy-start.6 = (f32[8,2,8,128]{3,2,1,0:T(8,128)S(1)}, f32[8,2,8,128]{3,2,1,0:T(8,128)}, u32[]{:S(2)}) copy-start(f32[8,2,8,128]{3,2,1,0:T(8,128)} %constant.12.clone.dir_ref) | copy-start | bytes 196612
  23.1 18.6 %collective-permute-start.2 = (f32[4,4096]{1,0:T(4,128)S(1)}, f32[4,4096]{1,0:T(4,128)S(1)}, u32[]{:S(2)}, u32[]{:S(2)}) collective-permute-start(f32[4,4096]{1,0:T(4,128)S(1)} %get-tuple-element.32), channel_id=1, source_target_pairs={{0,1},{1,2},{2,3},{3,4},{4,5},{5,6},{6,7},{7,0},{8,9},{9,10},{10,1... | collective-permute-start | bytes 196616 | tf_op jit(solution)/shard_map/ppermute | solution.py:658
  24.7 17.1 %collective-permute-start.3 = (f32[4,4096]{1,0:T(4,128)S(1)}, f32[4,4096]{1,0:T(4,128)S(1)}, u32[]{:S(2)}, u32[]{:S(2)}) collective-permute-start(f32[4,4096]{1,0:T(4,128)S(1)} %get-tuple-element.33), channel_id=1, source_target_pairs={{1,0},{2,1},{3,2},{4,3},{5,4},{6,5},{7,6},{0,7},{9,8},{10,9},{11,1... | collective-permute-start | bytes 196616 | tf_op jit(solution)/shard_map/ppermute | solution.py:658
  31.9 19.8 %all-to-all-start.1 = ((f32[128,1,128]{2,1,0:T(1,128)}), f32[128,1,128]{2,1,0:T(1,128)S(1)}, u32[]{:S(2)}, u32[]{:S(2)}) async-start(f32[128,1,128]{2,1,0:T(1,128)} %bitcast.2), calls=%async_computation.1 | async-start | bytes 131072 | tf_op jit(solution)/shard_map/all_to_all | solution.py:662
  49.6 36.8 %collective-permute-start.4 = (f32[4,4096]{1,0:T(4,128)S(1)}, f32[4,4096]{1,0:T(4,128)S(1)}, u32[]{:S(2)}, u32[]{:S(2)}) collective-permute-start(f32[4,4096]{1,0:T(4,128)S(1)} %get-tuple-element.35), channel_id=1, source_target_pairs={{0,1},{1,2},{2,3},{3,4},{4,5},{5,6},{6,7},{7,0},{8,9},{9,10},{10,1... | collective-permute-start | bytes 196616 | tf_op jit(solution)/shard_map/ppermute | solution.py:658
  51.1 35.4 %collective-permute-start.5 = (f32[4,4096]{1,0:T(4,128)S(1)}, f32[4,4096]{1,0:T(4,128)S(1)}, u32[]{:S(2)}, u32[]{:S(2)}) collective-permute-start(f32[4,4096]{1,0:T(4,128)S(1)} %get-tuple-element.36), channel_id=1, source_target_pairs={{1,0},{2,1},{3,2},{4,3},{5,4},{6,5},{7,6},{0,7},{9,8},{10,9},{11,1... | collective-permute-start | bytes 196616 | tf_op jit(solution)/shard_map/ppermute | solution.py:658
  51.6 13.5 %all-to-all-start.3 = ((f32[8,4,256]{2,1,0:T(4,128)}), f32[8,4,256]{2,1,0:T(4,128)S(1)}, u32[]{:S(2)}, u32[]{:S(2)}) async-start(f32[8,4,256]{2,1,0:T(4,128)} %get-tuple-element.45), calls=%async_computation.3 | async-start | bytes 65536 | tf_op jit(solution)/shard_map/all_to_all | solution.py:662
  58.2 0.7 copy-start.4
  58.2 0.7 copy-start.5
  65.1 12.4 %all-to-all-start.2 = ((f32[8,3,256]{2,1,0:T(4,128)}), f32[8,3,256]{2,1,0:T(4,128)S(1)}, u32[]{:S(2)}, u32[]{:S(2)}) async-start(f32[8,3,256]{2,1,0:T(4,128)} %kicks.2), calls=%async_computation.2 | async-start | bytes 65536 | tf_op jit(solution)/shard_map/all_to_all | solution.py:662
  77.5 18.4 %all-to-all-start.4 = ((f32[128,1,128]{2,1,0:T(1,128)}), f32[128,1,128]{2,1,0:T(1,128)S(1)}, u32[]{:S(2)}, u32[]{:S(2)}) async-start(f32[128,1,128]{2,1,0:T(1,128)} %bitcast.8), calls=%async_computation.4 | async-start | bytes 131072 | tf_op jit(solution)/shard_map/all_to_all | solution.py:662
  93.8 14.9 %collective-permute-start.6 = (f32[4,4096]{1,0:T(4,128)S(1)}, f32[4,4096]{1,0:T(4,128)S(1)}, u32[]{:S(2)}, u32[]{:S(2)}) collective-permute-start(f32[4,4096]{1,0:T(4,128)S(1)} %get-tuple-element.41), channel_id=1, source_target_pairs={{0,1},{1,2},{2,3},{3,4},{4,5},{5,6},{6,7},{7,0},{8,9},{9,10},{10,1... | collective-permute-start | bytes 196616 | tf_op jit(solution)/shard_map/ppermute | solution.py:658
  95.3 13.4 %collective-permute-start.7 = (f32[4,4096]{1,0:T(4,128)S(1)}, f32[4,4096]{1,0:T(4,128)S(1)}, u32[]{:S(2)}, u32[]{:S(2)}) collective-permute-start(f32[4,4096]{1,0:T(4,128)S(1)} %get-tuple-element.42), channel_id=1, source_target_pairs={{1,0},{2,1},{3,2},{4,3},{5,4},{6,5},{7,6},{0,7},{9,8},{10,9},{11,1... | collective-permute-start | bytes 196616 | tf_op jit(solution)/shard_map/ppermute | solution.py:658
  102.1 14.3 %all-to-all-start.5 = ((f32[8,3,256]{2,1,0:T(4,128)}), f32[8,3,256]{2,1,0:T(4,128)S(1)}, u32[]{:S(2)}, u32[]{:S(2)}) async-start(f32[8,3,256]{2,1,0:T(4,128)} %kicks.3), calls=%async_computation.5 | async-start | bytes 65536 | tf_op jit(solution)/shard_map/all_to_all | solution.py:662

commit v2 on v1

--- a/solution.py
+++ b/solution.py
@@ -154,7 +154,7 @@
     found.append(weight_ref[...])
     points = jnp.concatenate(found, axis=0)
     for part in range(PARTS):
-        point_ref[part] = points
+        point_ref[part, :, 0:SOL] = points
 
 
 def block_at(b):
@@ -193,10 +193,14 @@
     lax.fori_loop(0, NB, one_block, 0, unroll=FILL_UNROLL)
 
 
-def pair_kernel(step, kicked, gathers, last, *refs):
+def pair_kernel(step, kicked, gathers, last, merged, *refs):
     refs = list(refs)
     fourth_ref, position_ref, state_ref, left_ref, right_ref = refs[:5]
     refs = refs[5:]
+    if merged:
+        both_ref = left_ref
+        left_ref = both_ref.at[lax.rem(position_ref[0] + PARTS - 1, PARTS), :, SOL : SOL + HALO]
+        right_ref = both_ref.at[lax.rem(position_ref[0] + 1, PARTS), :, SOL : SOL + HALO]
     if kicked or gathers:
         index_ref, weight_ref = refs[:2]
         refs = refs[2:]
@@ -205,11 +209,12 @@
     if last:
         pos_ref, vel_ref = refs[:2]
         refs = refs[2:]
+    elif gathers:
+        out_ref, point_ref = refs[:2]
+        refs = refs[2:]
     else:
         out_ref, head_ref, tail_ref = refs[:3]
         refs = refs[3:]
-    if gathers:
-        point_ref = refs.pop(0)
     near_ref, moment_ref = refs[:2]
     refs = refs[2:]
     if gathers:
@@ -282,7 +287,13 @@
 
     lax.fori_loop(0, HB, one_pair, 0, unroll=BLOCK_UNROLL)
 
-    if not last:
+    if gathers:
+        position = position_ref[0]
+        up = lax.rem(position + 1, PARTS)
+        down = lax.rem(position + PARTS - 1, PARTS)
+        point_ref[down, :, SOL : SOL + HALO] = out_ref[0:4, 0:HALO]
+        point_ref[up, :, SOL : SOL + HALO] = out_ref[0:4, HALO:ATOMS]
+    elif not last:
         head_ref[...] = out_ref[0:4, 0:HALO]
         tail_ref[...] = out_ref[0:4, HALO:ATOMS]
     if gathers:
@@ -341,15 +352,16 @@
     ]
     if last:
         shapes = [jax.ShapeDtypeStruct((3, ATOMS), F32)] * 2
+    elif gathers:
+        shapes = [jax.ShapeDtypeStruct((8, ATOMS), F32), jax.ShapeDtypeStruct((PARTS, 4, SOL + HALO), F32)]
     else:
         shapes = [jax.ShapeDtypeStruct((8, ATOMS), F32)] + [jax.ShapeDtypeStruct((4, HALO), F32)] * 2
     if gathers:
-        shapes.append(jax.ShapeDtypeStruct((PARTS, 4, SOL), F32))
         scratch.append(pltpu.VMEM((3, NB, BLOCK), F32))
     if kicked:
         scratch.append(pltpu.VMEM((3, NB, BLOCK), F32))
     return pl.pallas_call(
-        functools.partial(pair_kernel, step, kicked, gathers, last),
+        functools.partial(pair_kernel, step, kicked, gathers, last, halo[0] is halo[1]),
         out_shape=shapes,
         in_specs=specs,
         out_specs=[VMEM] * len(shapes),
@@ -688,11 +700,11 @@
     halo = exchange(head, tail)
     amp, inten = amplitudes(position, first, directions)
     inten = to_all(inten, ("rep", "sp"))
-    state, head, tail, second = pair_step(
+    state, second = pair_step(
         1, tiles, position, state, halo, solute_index, scatter_weight, gathers=True
     )
-    halo = exchange(head, tail)
     second = to_all(second, "sp")
+    halo = (second, second)
     kick = to_all(kicks(position, first, directions, amp, inten, shells), "sp")
     amp, inten = amplitudes(position, second, directions)
     inten = to_all(inten, ("rep", "sp"))

time: 118 us -> 118 us (level)
  starting transfers between devices: 52.9 us -> 48.7 us
  waiting for transfers between devices: 3.73 us -> 7.22 us
    all_to_all x6, waiting for transfers between devices: 0.02 us -> 3.51 us  [to_all(): return lax.all_to_all(value, axes, 0, 0, tiled=True)]
    all_to_all x6, starting transfers between devices: 44.6 us -> 42.5 us  [to_all(): return lax.all_to_all(value, axes, 0, 0, tiled=True)]
    ppermute x8 -> x6, starting transfers between devices: 8.24 us -> 6.22 us  [exchange(): return (lax.ppermute(tail, 'sp', right), lax.ppermute(head, 'sp', left))]
    ppermute x8 -> x6, waiting for transfers between devices: 3.71 us -> 3.71 us  [exchange(): return (lax.ppermute(tail, 'sp', right), lax.ppermute(head, 'sp', left))]
  transfers between devices with their start and end apart: 14 -> 12, of which waited for: 2 -> 4; matrix products, arithmetic and copies ran while one was open for 1% -> 1% of each run, Pallas kernels for 47% -> 47%
where the time goes in v2:
time: 118 us; the launch traced here: 117 us
  Pallas kernels  56.4 us (48%)
  starting transfers between devices  48.7 us (41%)
  waiting for transfers between devices  7.22 us (6%)
  local copies, waits for them, and re-layouts  4 us (3%)
    all_to_all x6, starting transfers between devices, to_all(): return lax.all_to_all(value, axes, 0, 0, tiled=True)  42.5 us
    pallas_call x4, Pallas kernels, pair_step(): pl.pallas_call(functools.partial(pair_kernel, step, kicked, gathers, last...  29.2 us
    pallas_call x2, Pallas kernels, amplitudes(): pl.pallas_call(amplitude_kernel, grid_spec=pltpu.PrefetchScalarGridSpec(n...  13.3 us
    pallas_call x2, Pallas kernels, kicks(): pl.pallas_call(kick_kernel, grid_spec=pltpu.PrefetchScalarGridSpec(num_sc...  12.4 us
    ppermute x6, starting transfers between devices, exchange(): return (lax.ppermute(tail, 'sp', right), lax.ppermute(head, 'sp', left))  6.22 us
    unnamed x19, local copies, waits for them, and re-layouts  3.92 us
    ppermute x6, waiting for transfers between devices, exchange(): return (lax.ppermute(tail, 'sp', right), lax.ppermute(head, 'sp', left))  3.71 us
    all_to_all x6, waiting for transfers between devices, to_all(): return lax.all_to_all(value, axes, 0, 0, tiled=True)  3.51 us
  transfers between devices with their start and end apart: 12, of which 4 were waited for; matrix products, arithmetic and copies ran while one was open for 1% of the time, Pallas kernels for 47%

profile of v2, /device:TPU:8, one launch (start us, length us, event | category | flops | bytes accessed | tf_op | source)
XLA Modules:
  0.0 117.1 jit_solution(6643368142030951867)
XLA Ops:
  0.6 0.0 copy-start.1
  0.6 0.0 copy-start
  0.7 0.0 copy-start.3
  0.7 1.1 copy_bitcast_fusion
  1.8 0.0 copy-start.2
  1.8 0.0 copy-done.1
  1.8 0.0 copy-done
  1.8 0.0 copy-done.3
  1.8 0.6 copy-done.2
  2.4 0.0 copy-start.7
  2.4 1.0 pack.1
  3.5 1.6 %collective-permute-start = (f32[4,4096]{1,0:T(4,128)S(1)}, f32[4,4096]{1,0:T(4,128)S(1)}, u32[]{:S(2)}, u32[]{:S(2)}) collective-permute-start(f32[4,4096]{1,0:T(4,128)S(1)} %get-tuple-element.25), channel_id=1, source_target_pairs={{0,1},{1,2},{2,3},{3,4},{4,5},{5,6},{6,7},{7,0},{8,9},{9,10},{10,1... | collective-permute-start | bytes 196616 | tf_op jit(solution)/shard_map/ppermute | solution.py:670
  5.0 0.4 collective-permute-start.1
  5.5 0.0 copy-done.7
  5.5 0.1 sub.14.refs_0_
  5.6 2.1 %collective-permute-done.refs_3_ = f32[4,4096]{1,0:T(4,128)S(1)} collective-permute-done((f32[4,4096]{1,0:T(4,128)S(1)}, f32[4,4096]{1,0:T(4,128)S(1)}, u32[]{:S(2)}, u32[]{:S(2)}) %collective-permute-start) | collective-permute-done | bytes 65568 | tf_op jit(solution)/shard_map/ppermute | solution.py:670
  7.7 1.6 %collective-permute-done.1.refs_4_ = f32[4,4096]{1,0:T(4,128)S(1)} collective-permute-done((f32[4,4096]{1,0:T(4,128)S(1)}, f32[4,4096]{1,0:T(4,128)S(1)}, u32[]{:S(2)}, u32[]{:S(2)}) %collective-permute-start.1) | collective-permute-done | bytes 65568 | tf_op jit(solution)/shard_map/ppermute | solution.py:670
  9.3 6.8 %all-to-all-start.1 = ((f32[8,4,256]{2,1,0:T(4,128)}), f32[8,4,256]{2,1,0:T(4,128)S(1)}, u32[]{:S(2)}, u32[]{:S(2)}) async-start(f32[8,4,256]{2,1,0:T(4,128)} %get-tuple-element.34), calls=%async_computation.1 | async-start | bytes 65536 | tf_op jit(solution)/shard_map/all_to_all | solution.py:674
  16.2 0.0 copy-start.6
  16.2 7.0 %pair_step.4 = (f32[8,8192]{1,0:T(8,128)S(1)}, f32[4,4096]{1,0:T(4,128)S(1)}, f32[4,4096]{1,0:T(4,128)S(1)}) custom-call(s32[256]{0:T(256)S(1)} %sub.14.refs_0_, s32[1]{0:T(128)} %bitcast.refs_1_.position_ref, f32[8,8192]{1,0:T(8,128)S(1)} %get-tuple-element.23.refs_2_, f32[4,4096]{1,0:T(4,128)S(1)} %collective-permute-done.refs_3_, ...), custom_call_target="tpu_custom_call" | custom-call | flops 6000000000 | bytes 2000000 | tf_op jit(solution)/shard_map/pair_step/pallas_call | solution.py:363
  23.1 1.5 %collective-permute-start.2 = (f32[4,4096]{1,0:T(4,128)S(1)}, f32[4,4096]{1,0:T(4,128)S(1)}, u32[]{:S(2)}, u32[]{:S(2)}) collective-permute-start(f32[4,4096]{1,0:T(4,128)S(1)} %get-tuple-element.30), channel_id=1, source_target_pairs={{0,1},{1,2},{2,3},{3,4},{4,5},{5,6},{6,7},{7,0},{8,9},{9,10},{10,1... | collective-permute-start | bytes 196616 | tf_op jit(solution)/shard_map/ppermute | solution.py:670
  24.7 0.6 collective-permute-start.3
  25.2 0.0 all-to-all-done.1.point_ref
  25.2 0.0 copy-done.6
  25.2 6.6 %amplitudes.2 = (f32[13,4,8,128]{3,2,1,0:T(8,128)S(1)}, f32[128,128]{1,0:T(8,128)}) custom-call(s32[1]{0:T(128)} %bitcast.refs_1_.position_ref, f32[8,4,256]{2,1,0:T(4,128)S(1)} %all-to-all-done.1.point_ref, f32[8,2,8,128]{3,2,1,0:T(8,128)S(1)} %copy-done.6), custom_call_target="tpu_custom_call" | custom-call | flops 10000000000 | bytes 1000000 | tf_op jit(solution)/shard_map/amplitudes/pallas_call | solution.py:519
  31.9 9.9 %all-to-all-start.2 = ((f32[128,1,128]{2,1,0:T(1,128)}), f32[128,1,128]{2,1,0:T(1,128)S(1)}, u32[]{:S(2)}, u32[]{:S(2)}) async-start(f32[128,1,128]{2,1,0:T(1,128)} %bitcast.2), calls=%async_computation.2 | async-start | bytes 131072 | tf_op jit(solution)/shard_map/all_to_all | solution.py:674
  41.8 0.0 collective-permute-done.2.refs_3_
  41.8 0.0 collective-permute-done.3.refs_4_
  41.8 8.0 %pair_step.5 = (f32[8,8192]{1,0:T(8,128)S(1)}, f32[8,4,4352]{2,1,0:T(4,128)}) custom-call(s32[256]{0:T(256)S(1)} %sub.14.refs_0_, s32[1]{0:T(128)} %bitcast.refs_1_.position_ref, f32[8,8192]{1,0:T(8,128)S(1)} %get-tuple-element.29.refs_2_, f32[4,4096]{1,0:T(4,128)S(1)} %collective-permute-done.2.refs_3_, f32[4,4096]{1,0:T(4,128)S(1)} %collective-permute-done.3.refs_4_, ...), custom_call_target="tpu_custom_call" | custom-call | flops 6000000000 | bytes 2000000 | tf_op jit(solution)/shard_map/pair_step/pallas_call | solution.py:363
  49.8 0.8 all-to-all-done.2
  50.6 5.2 %all-to-all-start = ((f32[8,4,4352]{2,1,0:T(4,128)}), f32[8,4,4352]{2,1,0:T(4,128)S(1)}, u32[]{:S(2)}, u32[]{:S(2)}) async-start(f32[8,4,4352]{2,1,0:T(4,128)} %get-tuple-element.33), calls=%async_computation | async-start | bytes 1114112 | tf_op jit(solution)/shard_map/all_to_all | solution.py:674
  55.8 0.0 copy-start.4
  55.8 0.0 copy-start.5
  55.8 0.7 copy-done.4
  56.4 0.0 copy-done.5
  56.4 6.2 %kicks.2 = f32[8,3,256]{2,1,0:T(4,128)} custom-call(s32[1]{0:T(128)} %bitcast.refs_1_.position_ref, f32[8,4,256]{2,1,0:T(4,128)S(1)} %all-to-all-done.1.point_ref, f32[8,2,8,128]{3,2,1,0:T(8,128)S(1)} %copy-done.6, f32[13,4,8,128]{3,2,1,0:T(8,128)S(1)} %get-tuple-element.35.amp_ref, f32[128,128]{1,0:T(8,128)S(1)} %bitcast.19, f32[1,48]{1,0:T(1,128)S(1)} %bitcast.21, ...), custom_call_target="tpu_custom_call" | custom-call | flops 10000000000 | bytes 1000000 | tf_op jit(solution)/shard_map/kicks/pallas_call | solution.py:641
  62.6 2.7 %all-to-all-done.refs_3_.refs_4_.point_ref = f32[8,4,4352]{2,1,0:T(4,128)S(1)} async-done(((f32[8,4,4352]{2,1,0:T(4,128)}), f32[8,4,4352]{2,1,0:T(4,128)S(1)}, u32[]{:S(2)}, u32[]{:S(2)}) %all-to-all-start) | async-done | bytes 557088 | tf_op jit(solution)/shard_map/all_to_all | solution.py:674
  65.3 4.4 %all-to-all-start.3 = ((f32[8,3,256]{2,1,0:T(4,128)}), f32[8,3,256]{2,1,0:T(4,128)S(1)}, u32[]{:S(2)}, u32[]{:S(2)}) async-start(f32[8,3,256]{2,1,0:T(4,128)} %kicks.2), calls=%async_computation.3 | async-start | bytes 65536 | tf_op jit(solution)/shard_map/all_to_all | solution.py:674
  69.7 6.6 %amplitudes.3 = (f32[13,4,8,128]{3,2,1,0:T(8,128)S(1)}, f32[128,128]{1,0:T(8,128)}) custom-call(s32[1]{0:T(128)} %bitcast.refs_1_.position_ref, f32[8,4,4352]{2,1,0:T(4,128)S(1)} %all-to-all-done.refs_3_.refs_4_.point_ref, f32[8,2,8,128]{3,2,1,0:T(8,128)S(1)} %copy-done.6), custom_call_target="tpu_custom_call" | custom-call | flops 10000000000 | bytes 1000000 | tf_op jit(solution)/shard_map/amplitudes/pallas_call | solution.py:519
  76.4 0.0 all-to-all-done.3.refs_7_
  76.4 9.5 %all-to-all-start.4 = ((f32[128,1,128]{2,1,0:T(1,128)}), f32[128,1,128]{2,1,0:T(1,128)S(1)}, u32[]{:S(2)}, u32[]{:S(2)}) async-start(f32[128,1,128]{2,1,0:T(1,128)} %bitcast.8), calls=%async_computation.4 | async-start | bytes 131072 | tf_op jit(solution)/shard_map/all_to_all | solution.py:674
  85.9 7.3 %pair_step.6 = (f32[8,8192]{1,0:T(8,128)S(1)}, f32[4,4096]{1,0:T(4,128)S(1)}, f32[4,4096]{1,0:T(4,128)S(1)}) custom-call(s32[256]{0:T(256)S(1)} %sub.14.refs_0_, s32[1]{0:T(128)} %bitcast.refs_1_.position_ref, f32[8,8192]{1,0:T(8,128)S(1)} %get-tuple-element.32.refs_2_, f32[8,4,4352]{2,1,0:T(4,128)S(1)} %all-to-all-done.refs_3_.refs_4_.point_ref, ...), custom_call_target="tpu_custom_call" | custom-call | flops 6000000000 | bytes 2000000 | tf_op jit(solution)/shard_map/pair_step/pallas_call | solution.py:363
  93.3 1.5 %collective-permute-start.4 = (f32[4,4096]{1,0:T(4,128)S(1)}, f32[4,4096]{1,0:T(4,128)S(1)}, u32[]{:S(2)}, u32[]{:S(2)}) collective-permute-start(f32[4,4096]{1,0:T(4,128)S(1)} %get-tuple-element.38), channel_id=1, source_target_pairs={{0,1},{1,2},{2,3},{3,4},{4,5},{5,6},{6,7},{7,0},{8,9},{9,10},{10,1... | collective-permute-start | bytes 196616 | tf_op jit(solution)/shard_map/ppermute | solution.py:670
  94.8 0.6 collective-permute-start.5
  95.4 0.0 all-to-all-done.4
  95.4 6.2 %kicks.3 = f32[8,3,256]{2,1,0:T(4,128)} custom-call(s32[1]{0:T(128)} %bitcast.refs_1_.position_ref, f32[8,4,4352]{2,1,0:T(4,128)S(1)} %all-to-all-done.refs_3_.refs_4_.point_ref, f32[8,2,8,128]{3,2,1,0:T(8,128)S(1)} %copy-done.6, f32[13,4,8,128]{3,2,1,0:T(8,128)S(1)} %get-tuple-element.42.amp_ref, f32[128,128]{1,0:T(8,128)S(1)} %bitcast.20, ...), custom_call_target="tpu_custom_call" | custom-call | flops 10000000000 | bytes 1000000 | tf_op jit(solution)/shard_map/kicks/pallas_call | solution.py:641
  101.6 6.6 %all-to-all-start.5 = ((f32[8,3,256]{2,1,0:T(4,128)}), f32[8,3,256]{2,1,0:T(4,128)S(1)}, u32[]{:S(2)}, u32[]{:S(2)}) async-start(f32[8,3,256]{2,1,0:T(4,128)} %kicks.3), calls=%async_computation.5 | async-start | bytes 65536 | tf_op jit(solution)/shard_map/all_to_all | solution.py:674
  108.2 0.0 collective-permute-done.4.refs_3_
  108.2 0.0 collective-permute-done.5.refs_4_
  108.2 6.9 %pair_step.7 = (f32[3,8192]{1,0:T(4,128)S(1)}, f32[3,8192]{1,0:T(4,128)S(1)}) custom-call(s32[256]{0:T(256)S(1)} %sub.14.refs_0_, s32[1]{0:T(128)} %bitcast.refs_1_.position_ref, f32[8,8192]{1,0:T(8,128)S(1)} %get-tuple-element.37.refs_2_, f32[4,4096]{1,0:T(4,128)S(1)} %collective-permute-done.4.refs_3_, f32[4,4096]{1,0:T(4,128)S(1)} %collective-permute-done.5.refs_4_), custom_call_target="tpu_custom_call" | custom-call | flops 6000000000 | bytes 2000000 | tf_op jit(solution)/shard_map/pair_step/pallas_call | solution.py:363
  115.2 0.7 copy.16
  115.9 0.0 all-to-all-done.5.kick_ref
  115.9 0.4 finish.1
  116.4 0.7 copy.17
  (3 shorter events, 0.0 us)
Async XLA Ops:
  0.6 1.1 copy-start.1
  0.6 1.1 copy-start
  0.7 1.1 copy-start.3
  1.8 0.7 copy-start.2
  2.4 3.1 %copy-start.7 = (s32[1,4,64,4]{2,3,1,0:T(4,128)S(1)}, s32[1,4,64,4]{2,3,1,0:T(4,128)}, u32[]{:S(2)}) copy-start(s32[1,4,64,4]{2,3,1,0:T(4,128)} %param.14) | copy-start | bytes 12292
  3.5 4.3 %collective-permute-start = (f32[4,4096]{1,0:T(4,128)S(1)}, f32[4,4096]{1,0:T(4,128)S(1)}, u32[]{:S(2)}, u32[]{:S(2)}) collective-permute-start(f32[4,4096]{1,0:T(4,128)S(1)} %get-tuple-element.25), channel_id=1, source_target_pairs={{0,1},{1,2},{2,3},{3,4},{4,5},{5,6},{6,7},{7,0},{8,9},{9,10},{10,1... | collective-permute-start | bytes 196616 | tf_op jit(solution)/shard_map/ppermute | solution.py:670
  5.0 4.3 %collective-permute-start.1 = (f32[4,4096]{1,0:T(4,128)S(1)}, f32[4,4096]{1,0:T(4,128)S(1)}, u32[]{:S(2)}, u32[]{:S(2)}) collective-permute-start(f32[4,4096]{1,0:T(4,128)S(1)} %get-tuple-element.26), channel_id=1, source_target_pairs={{1,0},{2,1},{3,2},{4,3},{5,4},{6,5},{7,6},{0,7},{9,8},{10,9},{11,1... | collective-permute-start | bytes 196616 | tf_op jit(solution)/shard_map/ppermute | solution.py:670
  9.3 15.9 %all-to-all-start.1 = ((f32[8,4,256]{2,1,0:T(4,128)}), f32[8,4,256]{2,1,0:T(4,128)S(1)}, u32[]{:S(2)}, u32[]{:S(2)}) async-start(f32[8,4,256]{2,1,0:T(4,128)} %get-tuple-element.34), calls=%async_computation.1 | async-start | bytes 65536 | tf_op jit(solution)/shard_map/all_to_all | solution.py:674
  16.2 9.1 %copy-start.6 = (f32[8,2,8,128]{3,2,1,0:T(8,128)S(1)}, f32[8,2,8,128]{3,2,1,0:T(8,128)}, u32[]{:S(2)}) copy-start(f32[8,2,8,128]{3,2,1,0:T(8,128)} %constant.12.clone.dir_ref) | copy-start | bytes 196612
  23.1 18.6 %collective-permute-start.2 = (f32[4,4096]{1,0:T(4,128)S(1)}, f32[4,4096]{1,0:T(4,128)S(1)}, u32[]{:S(2)}, u32[]{:S(2)}) collective-permute-start(f32[4,4096]{1,0:T(4,128)S(1)} %get-tuple-element.30), channel_id=1, source_target_pairs={{0,1},{1,2},{2,3},{3,4},{4,5},{5,6},{6,7},{7,0},{8,9},{9,10},{10,1... | collective-permute-start | bytes 196616 | tf_op jit(solution)/shard_map/ppermute | solution.py:670
  24.7 17.1 %collective-permute-start.3 = (f32[4,4096]{1,0:T(4,128)S(1)}, f32[4,4096]{1,0:T(4,128)S(1)}, u32[]{:S(2)}, u32[]{:S(2)}) collective-permute-start(f32[4,4096]{1,0:T(4,128)S(1)} %get-tuple-element.31), channel_id=1, source_target_pairs={{1,0},{2,1},{3,2},{4,3},{5,4},{6,5},{7,6},{0,7},{9,8},{10,9},{11,1... | collective-permute-start | bytes 196616 | tf_op jit(solution)/shard_map/ppermute | solution.py:670
  31.9 18.7 %all-to-all-start.2 = ((f32[128,1,128]{2,1,0:T(1,128)}), f32[128,1,128]{2,1,0:T(1,128)S(1)}, u32[]{:S(2)}, u32[]{:S(2)}) async-start(f32[128,1,128]{2,1,0:T(1,128)} %bitcast.2), calls=%async_computation.2 | async-start | bytes 131072 | tf_op jit(solution)/shard_map/all_to_all | solution.py:674
  50.6 14.7 %all-to-all-start = ((f32[8,4,4352]{2,1,0:T(4,128)}), f32[8,4,4352]{2,1,0:T(4,128)S(1)}, u32[]{:S(2)}, u32[]{:S(2)}) async-start(f32[8,4,4352]{2,1,0:T(4,128)} %get-tuple-element.33), calls=%async_computation | async-start | bytes 1114112 | tf_op jit(solution)/shard_map/all_to_all | solution.py:674
  55.8 0.7 copy-start.4
  55.8 0.7 copy-start.5
  65.3 11.1 %all-to-all-start.3 = ((f32[8,3,256]{2,1,0:T(4,128)}), f32[8,3,256]{2,1,0:T(4,128)S(1)}, u32[]{:S(2)}, u32[]{:S(2)}) async-start(f32[8,3,256]{2,1,0:T(4,128)} %kicks.2), calls=%async_computation.3 | async-start | bytes 65536 | tf_op jit(solution)/shard_map/all_to_all | solution.py:674
  76.4 19.0 %all-to-all-start.4 = ((f32[128,1,128]{2,1,0:T(1,128)}), f32[128,1,128]{2,1,0:T(1,128)S(1)}, u32[]{:S(2)}, u32[]{:S(2)}) async-start(f32[128,1,128]{2,1,0:T(1,128)} %bitcast.8), calls=%async_computation.4 | async-start | bytes 131072 | tf_op jit(solution)/shard_map/all_to_all | solution.py:674
  93.3 14.9 %collective-permute-start.4 = (f32[4,4096]{1,0:T(4,128)S(1)}, f32[4,4096]{1,0:T(4,128)S(1)}, u32[]{:S(2)}, u32[]{:S(2)}) collective-permute-start(f32[4,4096]{1,0:T(4,128)S(1)} %get-tuple-element.38), channel_id=1, source_target_pairs={{0,1},{1,2},{2,3},{3,4},{4,5},{5,6},{6,7},{7,0},{8,9},{9,10},{10,1... | collective-permute-start | bytes 196616 | tf_op jit(solution)/shard_map/ppermute | solution.py:670
  94.8 13.4 %collective-permute-start.5 = (f32[4,4096]{1,0:T(4,128)S(1)}, f32[4,4096]{1,0:T(4,128)S(1)}, u32[]{:S(2)}, u32[]{:S(2)}) collective-permute-start(f32[4,4096]{1,0:T(4,128)S(1)} %get-tuple-element.39), channel_id=1, source_target_pairs={{1,0},{2,1},{3,2},{4,3},{5,4},{6,5},{7,6},{0,7},{9,8},{10,9},{11,1... | collective-permute-start | bytes 196616 | tf_op jit(solution)/shard_map/ppermute | solution.py:670
  101.6 14.3 %all-to-all-start.5 = ((f32[8,3,256]{2,1,0:T(4,128)}), f32[8,3,256]{2,1,0:T(4,128)S(1)}, u32[]{:S(2)}, u32[]{:S(2)}) async-start(f32[8,3,256]{2,1,0:T(4,128)} %kicks.3), calls=%async_computation.5 | async-start | bytes 65536 | tf_op jit(solution)/shard_map/all_to_all | solution.py:674
